TPU v7x, 32 devices: a whole 2x2x4 slice. The times are simulated.
32 devices in a mesh: gx: 2 (over x), gy: 4 (over y, core), gz: 4 (over z).
Axes of the slice: x: 2, y: 2, z: 4, core: 2. Of those that a mesh axis runs over, the one named last changes fastest.
Arguments:
- velocity: float32 [3, 32, 64, 512], P(None, 'gx', 'gy', 'gz'), may hold values from -6 to 6
- gradients: bfloat16 [2, 3, 32, 64, 512], P(None, None, 'gx', 'gy', 'gz'), may hold values from -6 to 6
- shift_x: int32 [2, 4, 8, 4], P(None, 'gx', 'gy', 'gz'), may hold values from -6 to 6
- shift_y: int32 [2, 4, 8, 4], P(None, 'gx', 'gy', 'gz'), may hold values from -6 to 6
- shift_z: int32 [2, 4, 8, 4], P(None, 'gx', 'gy', 'gz'), may hold values from -14 to 14
- fractions: int32 [2, 3, 4, 8, 4], P(None, None, 'gx', 'gy', 'gz'), may hold values from 0 to 7
Outputs:
- hess_vec: float32 [3, 32, 64, 512], P(None, 'gx', 'gy', 'gz')
All inputs are finite; a program needn't handle non-finite values.
Results may differ from a plain program's by a relative error of at most 0.0003.
Values sent between devices are 32-bit elements; how exact they have to be, the bound alone decides.
A program may use at most 64 MiB of HBM per device.

v0:
```python
import jax
import jax.numpy as jnp
from jax import lax
from jax.sharding import PartitionSpec as P

BX = 8
BY = 8
BZ = 128
RX = 6
RY = 6
RZ = 14
STEPS = 2


STEP_SIZE = 0.5
REG_WEIGHT = 0.1
LAPLACE_TAPS = (-205.0 / 72.0, 8.0 / 5.0, -1.0 / 5.0, 8.0 / 315.0, -1.0 / 560.0)


def with_halo(shard, sides, width):
    for axis, dim in sides:
        count, length = (lax.axis_size(axis), shard.shape[dim])
        up = [(i, (i + 1) % count) for i in range(count - 1)]
        down = [(j, i) for i, j in up]
        last = lax.slice_in_dim(shard, length - width, length, axis=dim)
        initial = lax.slice_in_dim(shard, 0, width, axis=dim)
        before = lax.ppermute(last, axis, up)
        after = lax.ppermute(initial, axis, down)
        shard = jnp.concatenate([before, shard, after], axis=dim)
    return shard


def cubic_weights(fractions):
    fraction = fractions.astype(jnp.float32) / 8.0
    squared = fraction * fraction
    cubed = squared * fraction
    taps = jnp.stack(
        [
            0.5 * (2.0 * squared - cubed - fraction),
            0.5 * (3.0 * cubed - 5.0 * squared + 2.0),
            0.5 * (4.0 * squared - 3.0 * cubed + fraction),
            0.5 * (cubed - squared),
        ],
        axis=-1,
    )
    return taps.reshape(3, -1, 4)


def block_starts(shift_x, shift_y, shift_z):
    count_x, count_y, count_z = shift_x.shape
    base_x = jnp.arange(count_x, dtype=jnp.int32)[:, None, None] * BX
    base_y = jnp.arange(count_y, dtype=jnp.int32)[None, :, None] * BY
    base_z = jnp.arange(count_z, dtype=jnp.int32)[None, None, :] * BZ
    start_x = (base_x + shift_x + (RX + 1)).reshape(-1)
    start_y = (base_y + shift_y + (RY + 1)).reshape(-1)
    start_z = (base_z + shift_z + (RZ + 1)).reshape(-1)
    return (start_x, start_y, start_z)


def to_blocks(field):
    tile_x, tile_y, tile_z = field.shape
    split = field.reshape(tile_x // BX, BX, tile_y // BY, BY, tile_z // BZ, BZ)
    return split.transpose(0, 2, 4, 1, 3, 5).reshape(-1, BX, BY, BZ)


def from_blocks(blocks, tile_x, tile_y, tile_z):
    split = blocks.reshape(tile_x // BX, tile_y // BY, tile_z // BZ, BX, BY, BZ)
    return split.transpose(0, 3, 1, 4, 2, 5).reshape(tile_x, tile_y, tile_z)


def spread_blocks(field, start_x, start_y, start_z, weights):
    values = to_blocks(field)
    accumulated = jnp.zeros(
        (
            field.shape[0] + 2 * (RX + 2),
            field.shape[1] + 2 * (RY + 2),
            field.shape[2] + 2 * (RZ + 2),
        ),
        jnp.float32,
    )

    def add_block(b, accumulated):
        weight_x = weights[0, b]
        weight_y = weights[1, b]
        weight_z = weights[2, b]
        block_vals = values[b]
        along_x = sum(
            (weight_x[a] * jnp.pad(block_vals, ((a, 3 - a), (0, 0), (0, 0))) for a in range(4))
        )
        along_y = sum(
            (weight_y[a] * jnp.pad(along_x, ((0, 0), (a, 3 - a), (0, 0))) for a in range(4))
        )
        for a in range(4):
            corner = (start_x[b], start_y[b], start_z[b] + a)
            current = lax.dynamic_slice(accumulated, corner, along_y.shape)
            accumulated = lax.dynamic_update_slice(
                accumulated, current + weight_z[a] * along_y, corner
            )
        return accumulated

    return lax.fori_loop(0, values.shape[0], add_block, accumulated)


def neg_laplacian(padded):
    tile_x = padded.shape[1] - 8
    tile_y = padded.shape[2] - 8
    tile_z = padded.shape[3] - 8

    def shifted(off_x, off_y, off_z):
        return padded[
            :,
            4 + off_x : 4 + off_x + tile_x,
            4 + off_y : 4 + off_y + tile_y,
            4 + off_z : 4 + off_z + tile_z,
        ]

    result = 3.0 * LAPLACE_TAPS[0] * shifted(0, 0, 0)
    for k in range(1, 5):
        result = result + LAPLACE_TAPS[k] * (
            shifted(k, 0, 0)
            + shifted(-k, 0, 0)
            + shifted(0, k, 0)
            + shifted(0, -k, 0)
            + shifted(0, 0, k)
            + shifted(0, 0, -k)
        )
    return -result


def departure(source, widths):
    wide_x, wide_y, wide_z = widths
    deepest = max(widths)
    widened = with_halo(source, (("gx", 0), ("gy", 1), ("gz", 2)), deepest)
    first = (deepest - wide_x, deepest - wide_y, deepest - wide_z)
    last = (
        deepest + source.shape[0] + wide_x,
        deepest + source.shape[1] + wide_y,
        deepest + source.shape[2] + wide_z,
    )
    return lax.slice(widened, first, last)


def rim_pair(accumulated, dim, width):
    extent = accumulated.shape[dim]
    low_rim = lax.slice_in_dim(accumulated, 0, width, axis=dim)
    high_rim = lax.slice_in_dim(accumulated, extent - width, extent, axis=dim)
    return jnp.concatenate([low_rim, high_rim], axis=dim)


def fold_rim(accumulated, dim, width, outer_rims):
    extent = accumulated.shape[dim]
    interior = lax.slice_in_dim(accumulated, width, extent - width, axis=dim)
    inner_len = extent - 2 * width
    from_below = lax.slice_in_dim(outer_rims, 0, width, axis=dim)
    from_above = lax.slice_in_dim(outer_rims, 3 * width, 4 * width, axis=dim)
    padding = [(0, 0), (0, 0), (0, 0)]
    padding[dim] = (0, inner_len - width)
    low_part = jnp.pad(from_below, padding)
    padding[dim] = (inner_len - width, 0)
    return interior + low_part + jnp.pad(from_above, padding)


def return_rims(accumulated, widths):
    wide_x, wide_y, wide_z = widths
    accumulated = fold_rim(
        accumulated, 0, wide_x, with_halo(rim_pair(accumulated, 0, wide_x), (("gx", 0),), wide_x)
    )
    accumulated = fold_rim(
        accumulated, 1, wide_y, with_halo(rim_pair(accumulated, 1, wide_y), (("gy", 1),), wide_y)
    )
    return fold_rim(
        accumulated, 2, wide_z, with_halo(rim_pair(accumulated, 2, wide_z), (("gz", 2),), wide_z)
    )


def body(velocity, gradients, shift_x, shift_y, shift_z, fractions):
    widths = (RX + 2, RY + 2, RZ + 2)
    tile_x, tile_y, tile_z = (velocity.shape[1], velocity.shape[2], velocity.shape[3])
    faces = with_halo(velocity, (("gx", 1), ("gy", 2), ("gz", 3)), 4)
    regular = REG_WEIGHT * neg_laplacian(faces)
    state = jnp.zeros((tile_x, tile_y, tile_z), jnp.float32)
    for k in range(STEPS):
        source = state + STEP_SIZE * jnp.sum(gradients[k].astype(jnp.float32) * velocity, axis=0)
        padded = departure(source, widths)
        start_x, start_y, start_z = block_starts(shift_x[k], shift_y[k], shift_z[k])
        weights = cubic_weights(fractions[k])

        def one_block(corner_x, corner_y, corner_z, weight_x, weight_y, weight_z):
            along_z = sum(
                (
                    weight_z[a]
                    * lax.dynamic_slice(
                        padded, (corner_x, corner_y, corner_z + a), (BX + 3, BY + 3, BZ)
                    )
                    for a in range(4)
                )
            )
            along_y = sum((weight_y[a] * along_z[:, a : a + BY, :] for a in range(4)))
            return sum((weight_x[a] * along_y[a : a + BX] for a in range(4)))

        blocks = jax.vmap(one_block)(start_x, start_y, start_z, weights[0], weights[1], weights[2])
        state = from_blocks(blocks, tile_x, tile_y, tile_z)
    adjoint = state
    gauss_term = jnp.zeros_like(velocity)
    for k in reversed(range(STEPS)):
        start_x, start_y, start_z = block_starts(shift_x[k], shift_y[k], shift_z[k])
        weights = cubic_weights(fractions[k])
        accumulated = spread_blocks(adjoint, start_x, start_y, start_z, weights)
        adjoint = return_rims(accumulated, widths)
        gauss_term = gauss_term + STEP_SIZE * gradients[k].astype(jnp.float32) * adjoint[None]
    return regular + gauss_term


def solution(mesh):
    in_specs = (
        P(None, "gx", "gy", "gz"),
        P(None, None, "gx", "gy", "gz"),
        P(None, "gx", "gy", "gz"),
        P(None, "gx", "gy", "gz"),
        P(None, "gx", "gy", "gz"),
        P(None, None, "gx", "gy", "gz"),
    )
    out_specs = P(None, "gx", "gy", "gz")
    return jax.shard_map(body, mesh=mesh, in_specs=in_specs, out_specs=out_specs, check_vma=False)
```

profile of v0, /device:TPU:0, one launch (start us, length us, event | category | flops | bytes accessed | tf_op | source)
XLA Modules:
  0.0 642.1 jit_solution(1806942885416021116)
XLA Ops:
  3.0 5.5 collective-permute-start.1
  22.7 4.6 collective-permute-start.6
  40.2 5.3 collective-permute-start.10
  54.7 14.0 %while.42 = (s32[]{:T(128)}, f32[32,32,160]{2,1,0:T(8,128)S(1)}, s32[4,3]{1,0:T(4,128)}, f32[4,11,11,128]{3,2,1,0:T(8,128)S(1)}, s32[]{:T(128)}) while((s32[]{:T(128)}, f32[32,32,160]{2,1,0:T(8,128)S(1)}, s32[4,3]{1,0:T(4,128)}, f32[4,11,11,128]{3,2,1,0:T(8,128)S(1)}, s32[]{:T(128)}) %tuple.412), condition=%wide.while_cond.2, body=%wide.while_body.2.sunk | while | flops 2 | bytes 180361 | solution.py:192
  68.8 13.5 %while.41 = (s32[]{:T(128)}, f32[32,32,160]{2,1,0:T(8,128)S(1)}, s32[4,3]{1,0:T(4,128)}, f32[4,11,11,128]{3,2,1,0:T(8,128)S(1)}, s32[]{:T(128)}) while((s32[]{:T(128)}, f32[32,32,160]{2,1,0:T(8,128)S(1)}, s32[4,3]{1,0:T(4,128)}, f32[4,11,11,128]{3,2,1,0:T(8,128)S(1)}, s32[]{:T(128)}) %tuple.439), condition=%wide.while_cond.1, body=%wide.while_body.1.sunk | while | flops 2 | bytes 180361 | solution.py:192
  82.4 13.5 %while.40 = (s32[]{:T(128)}, f32[32,32,160]{2,1,0:T(8,128)S(1)}, s32[4,3]{1,0:T(4,128)}, f32[4,11,11,128]{3,2,1,0:T(8,128)S(1)}, s32[]{:T(128)}) while((s32[]{:T(128)}, f32[32,32,160]{2,1,0:T(8,128)S(1)}, s32[4,3]{1,0:T(4,128)}, f32[4,11,11,128]{3,2,1,0:T(8,128)S(1)}, s32[]{:T(128)}) %tuple.440), condition=%wide.while_cond, body=%wide.while_body.sunk | while | flops 2 | bytes 180361 | solution.py:192
  96.6 15.8 %while.43 = (s32[]{:T(128)}, f32[32,32,160]{2,1,0:T(8,128)S(1)}, s32[4,3]{1,0:T(4,128)}, f32[4,11,11,128]{3,2,1,0:T(8,128)}, s32[]{:T(128)}) while((s32[]{:T(128)}, f32[32,32,160]{2,1,0:T(8,128)S(1)}, s32[4,3]{1,0:T(4,128)}, f32[4,11,11,128]{3,2,1,0:T(8,128)}, s32[]{:T(128)}) %tuple.441), condition=%wide.while_cond.3, body=%wide.while_body.3.sunk | while | flops 2 | bytes 153725 | solution.py:192
  115.9 4.6 collective-permute-start.12
  124.3 5.3 collective-permute-start.14
  135.7 4.7 collective-permute-start.16
  149.1 10.9 %while.46 = (s32[]{:T(128)}, f32[32,32,160]{2,1,0:T(8,128)S(1)}, s32[4,3]{1,0:T(4,128)S(1)}, f32[4,11,11,128]{3,2,1,0:T(8,128)S(1)}, s32[]{:T(128)}) while((s32[]{:T(128)}, f32[32,32,160]{2,1,0:T(8,128)S(1)}, s32[4,3]{1,0:T(4,128)S(1)}, f32[4,11,11,128]{3,2,1,0:T(8,128)S(1)}, s32[]{:T(128)}) %tuple.424), condition=%wide.while_cond.6, body=%wide.while_body.6.sunk | while | flops 2 | bytes 180361 | solution.py:192
  160.1 10.6 %while.45 = (s32[]{:T(128)}, f32[32,32,160]{2,1,0:T(8,128)S(1)}, s32[4,3]{1,0:T(4,128)S(1)}, f32[4,11,11,128]{3,2,1,0:T(8,128)S(1)}, s32[]{:T(128)}) while((s32[]{:T(128)}, f32[32,32,160]{2,1,0:T(8,128)S(1)}, s32[4,3]{1,0:T(4,128)S(1)}, f32[4,11,11,128]{3,2,1,0:T(8,128)S(1)}, s32[]{:T(128)}) %tuple.442), condition=%wide.while_cond.5, body=%wide.while_body.5.sunk | while | flops 2 | bytes 180361 | solution.py:192
  170.8 10.6 %while.44 = (s32[]{:T(128)}, f32[32,32,160]{2,1,0:T(8,128)S(1)}, s32[4,3]{1,0:T(4,128)S(1)}, f32[4,11,11,128]{3,2,1,0:T(8,128)S(1)}, s32[]{:T(128)}) while((s32[]{:T(128)}, f32[32,32,160]{2,1,0:T(8,128)S(1)}, s32[4,3]{1,0:T(4,128)S(1)}, f32[4,11,11,128]{3,2,1,0:T(8,128)S(1)}, s32[]{:T(128)}) %tuple.443), condition=%wide.while_cond.4, body=%wide.while_body.4.sunk | while | flops 2 | bytes 180361 | solution.py:192
  182.1 13.2 %while.47 = (s32[]{:T(128)}, f32[32,32,160]{2,1,0:T(8,128)S(1)}, s32[4,3]{1,0:T(4,128)S(1)}, f32[4,11,11,128]{3,2,1,0:T(8,128)}, s32[]{:T(128)}) while((s32[]{:T(128)}, f32[32,32,160]{2,1,0:T(8,128)S(1)}, s32[4,3]{1,0:T(4,128)S(1)}, f32[4,11,11,128]{3,2,1,0:T(8,128)}, s32[]{:T(128)}) %tuple.444), condition=%wide.while_cond.7, body=%wide.while_body.7.sunk | while | flops 2 | bytes 153725 | solution.py:192
  197.2 175.1 %while.38 = (s32[]{:T(128)}, f32[32,32,160]{2,1,0:T(8,128)S(1)}, s32[4]{0:T(128)S(1)}, s32[4]{0:T(128)S(1)}, s32[4]{0:T(128)S(1)}, /*index=5*/f32[3,4,4]{2,1,0:T...) while((s32[]{:T(128)}, f32[32,32,160]{2,1,0:T(8,128)S(1)}, ...), condition=%wide.region_3.4_spmd, body=%wide.region_2.3_spmd.sunk | while | flops 636439 | bytes 1315609 | solution.py:101
  215.7 3.9 dynamic_update_slice.88
  230.1 3.9 dynamic_update_slice.90
  237.3 3.9 dynamic_update_slice.91
  372.4 4.8 collective-permute-start.18
  381.0 4.4 collective-permute-done.19
  385.5 7.9 %collective-permute-start.20 = (f32[16,8,160]{2,1,0:T(8,128)S(1)}, f32[16,8,160]{2,1,0:T(8,128)S(1)}, u32[]{:S(2)}, u32[]{:S(2)}) collective-permute-start(f32[16,8,160]{2,1,0:T(8,128)S(1)} %get-tuple-element.1059), channel_id=1, source_target_pairs={{0,4},{4,8},{8,12},{1,5},{5,9},{9,13},{2,6},{6,10},{10,14},{3,7},{... | collective-permute-start | bytes 245768 | tf_op jit(solution)/shard_map/ppermute | solution.py:27
  394.8 7.1 %collective-permute-start.3 = (f32[3,24,4,128]{3,1,2,0:T(8,128)S(1)}, f32[3,24,4,128]{3,1,2,0:T(8,128)S(1)}, u32[]{:S(2)}, u32[]{:S(2)}) collective-permute-start(f32[3,24,4,128]{3,1,2,0:T(8,128)S(1)} %copy.408), channel_id=1, source_target_pairs={{0,4},{4,8},{8,12},{1,5},{5,9},{9,13},{2,6},{6,10},{10,14},{3,7},{... | collective-permute-start | bytes 442376 | tf_op jit(solution)/shard_map/ppermute | solution.py:27
  403.3 4.5 collective-permute-start.22
  420.4 174.5 %while.39 = (s32[]{:T(128)}, f32[32,32,160]{2,1,0:T(8,128)S(1)}, s32[4]{0:T(128)S(1)}, s32[4]{0:T(128)S(1)}, s32[4]{0:T(128)S(1)}, /*index=5*/f32[3,4,4]{2,1,0:T...) while((s32[]{:T(128)}, f32[32,32,160]{2,1,0:T(8,128)S(1)}, ...), condition=%wide.region_5.6_spmd, body=%wide.region_4.5_spmd.sunk | while | flops 636439 | bytes 1315609 | solution.py:101
  439.0 4.0 dynamic_update_slice.92
  446.1 4.0 dynamic_update_slice.93
  453.2 4.0 dynamic_update_slice.94
  460.3 4.0 dynamic_update_slice.95
  598.3 7.6 %pad_maximum_fusion = f32[3,24,24,128]{2,1,3,0:T(8,128)S(1)} fusion(f32[3,24,4,128]{2,1,3,0:T(8,128)} %copy.370, f32[3,24,16,128]{2,1,3,0:T(8,128)} %copy.369, f32[3,24,4,128]{2,1,3,0:T(8,128)} %copy.368), kind=kLoop, calls=%fused_computation.36 | loop fusion | flops 442368 | bytes 1769472 | tf_op jit(solution)/shard_map/concatenate | solution.py:29
  613.2 5.9 collective-permute-start.5
  625.2 4.6 copy.371
  636.2 5.8 fusion.2
  (502 shorter events, 452.5 us)
Async XLA Ops:
  1.7 377.0 %collective-permute-start = (f32[3,4,16,128]{3,2,1,0:T(8,128)}, f32[3,4,16,128]{3,2,1,0:T(8,128)}, u32[]{:S(2)}, u32[]{:S(2)}) collective-permute-start(f32[3,4,16,128]{3,2,1,0:T(8,128)} %get-tuple-element.1064), channel_id=1, source_target_pairs={{16,0},{17,1},{18,2},{19,3},{20,4},{21,5},{22,6},{23,7},{24,8},{25... | collective-permute-start | bytes 294920 | tf_op jit(solution)/shard_map/ppermute | solution.py:28
  3.0 16.7 %collective-permute-start.1 = (f32[3,4,16,128]{3,2,1,0:T(8,128)S(1)}, f32[3,4,16,128]{3,2,1,0:T(8,128)S(1)}, u32[]{:S(2)}, u32[]{:S(2)}) collective-permute-start(f32[3,4,16,128]{3,2,1,0:T(8,128)S(1)} %get-tuple-element.1065), channel_id=1, source_target_pairs={{0,16},{1,17},{2,18},{3,19},{4,20},{5,21},{6,22},{7,23},{8,24},{9,... | collective-permute-start | bytes 294920 | tf_op jit(solution)/shard_map/ppermute | solution.py:27
  21.4 7.7 %collective-permute-start.7 = (f32[16,16,128]{2,1,0:T(8,128)S(1)}, f32[16,16,128]{2,1,0:T(8,128)S(1)}, u32[]{:S(2)}, u32[]{:S(2)}) collective-permute-start(f32[16,16,128]{2,1,0:T(8,128)S(1)} %broadcast_multiply_fusion.1), channel_id=1, source_target_pairs={{16,0},{17,1},{18,2},{19,3},{20,4},{21,5},{22,6},{23,7},{24,8},{25... | collective-permute-start | bytes 393224 | tf_op jit(solution)/shard_map/ppermute | solution.py:28
  22.7 7.1 %collective-permute-start.6 = (f32[16,16,128]{2,1,0:T(8,128)S(1)}, f32[16,16,128]{2,1,0:T(8,128)S(1)}, u32[]{:S(2)}, u32[]{:S(2)}) collective-permute-start(f32[16,16,128]{2,1,0:T(8,128)S(1)} %broadcast_multiply_fusion.1), channel_id=1, source_target_pairs={{0,16},{1,17},{2,18},{3,19},{4,20},{5,21},{6,22},{7,23},{8,24},{9,... | collective-permute-start | bytes 393224 | tf_op jit(solution)/shard_map/ppermute | solution.py:27
  29.8 4.9 collective-permute-start.9
  31.1 4.4 collective-permute-start.8
  38.9 12.8 %collective-permute-start.11 = (f32[48,48,16]{1,2,0:T(8,128)}, f32[48,48,16]{1,2,0:T(8,128)S(1)}, u32[]{:S(2)}, u32[]{:S(2)}) collective-permute-start(f32[48,48,16]{1,2,0:T(8,128)} %copy.410), channel_id=1, source_target_pairs={{1,0},{2,1},{3,2},{5,4},{6,5},{7,6},{9,8},{10,9},{11,10},{13,12},{... | collective-permute-start | bytes 442376 | tf_op jit(solution)/shard_map/ppermute | solution.py:28
  40.2 11.1 %collective-permute-start.10 = (f32[48,48,16]{1,2,0:T(8,128)S(1)}, f32[48,48,16]{1,2,0:T(8,128)S(1)}, u32[]{:S(2)}, u32[]{:S(2)}) collective-permute-start(f32[48,48,16]{1,2,0:T(8,128)S(1)} %copy-done.19), channel_id=1, source_target_pairs={{0,1},{1,2},{2,3},{4,5},{5,6},{6,7},{8,9},{9,10},{10,11},{12,13},{... | collective-permute-start | bytes 442376 | tf_op jit(solution)/shard_map/ppermute | solution.py:27
  82.3 30.1 %copy-start.21 = (f32[4]{0:T(128)S(1)}, f32[4]{0:T(128)}, u32[]{:S(2)}) copy-start(f32[4]{0:T(128)} %get-tuple-element.881) | copy-start | bytes 52
  114.6 6.9 %collective-permute-start.13 = (f32[16,16,128]{2,1,0:T(8,128)S(1)}, f32[16,16,128]{2,1,0:T(8,128)S(1)}, u32[]{:S(2)}, u32[]{:S(2)}) collective-permute-start(f32[16,16,128]{2,1,0:T(8,128)S(1)} %multiply_add_fusion.14), channel_id=1, source_target_pairs={{16,0},{17,1},{18,2},{19,3},{20,4},{21,5},{22,6},{23,7},{24,8},{25... | collective-permute-start | bytes 393224 | tf_op jit(solution)/shard_map/ppermute | solution.py:28
  115.9 7.1 %collective-permute-start.12 = (f32[16,16,128]{2,1,0:T(8,128)S(1)}, f32[16,16,128]{2,1,0:T(8,128)S(1)}, u32[]{:S(2)}, u32[]{:S(2)}) collective-permute-start(f32[16,16,128]{2,1,0:T(8,128)S(1)} %multiply_add_fusion.14), channel_id=1, source_target_pairs={{0,16},{1,17},{2,18},{3,19},{4,20},{5,21},{6,22},{7,23},{8,24},{9,... | collective-permute-start | bytes 393224 | tf_op jit(solution)/shard_map/ppermute | solution.py:27
  123.0 7.1 %collective-permute-start.15 = (f32[48,16,128]{2,1,0:T(8,128)S(1)}, f32[48,16,128]{2,1,0:T(8,128)S(1)}, u32[]{:S(2)}, u32[]{:S(2)}) collective-permute-start(f32[48,16,128]{2,1,0:T(8,128)S(1)} %pad_maximum_fusion.20), channel_id=1, source_target_pairs={{4,0},{8,4},{12,8},{5,1},{9,5},{13,9},{6,2},{10,6},{14,10},{7,3},{... | collective-permute-start | bytes 1179656 | tf_op jit(solution)/shard_map/ppermute | solution.py:28
  124.3 6.6 %collective-permute-start.14 = (f32[48,16,128]{2,1,0:T(8,128)S(1)}, f32[48,16,128]{2,1,0:T(8,128)S(1)}, u32[]{:S(2)}, u32[]{:S(2)}) collective-permute-start(f32[48,16,128]{2,1,0:T(8,128)S(1)} %pad_maximum_fusion.20), channel_id=1, source_target_pairs={{0,4},{4,8},{8,12},{1,5},{5,9},{9,13},{2,6},{6,10},{10,14},{3,7},{... | collective-permute-start | bytes 1179656 | tf_op jit(solution)/shard_map/ppermute | solution.py:27
  134.4 11.7 %collective-permute-start.17 = (f32[48,48,16]{1,2,0:T(8,128)}, f32[48,48,16]{1,2,0:T(8,128)S(1)}, u32[]{:S(2)}, u32[]{:S(2)}) collective-permute-start(f32[48,48,16]{1,2,0:T(8,128)} %copy.412), channel_id=1, source_target_pairs={{1,0},{2,1},{3,2},{5,4},{6,5},{7,6},{9,8},{10,9},{11,10},{13,12},{... | collective-permute-start | bytes 442376 | tf_op jit(solution)/shard_map/ppermute | solution.py:28
  135.7 10.0 %collective-permute-start.16 = (f32[48,48,16]{1,2,0:T(8,128)S(1)}, f32[48,48,16]{1,2,0:T(8,128)S(1)}, u32[]{:S(2)}, u32[]{:S(2)}) collective-permute-start(f32[48,48,16]{1,2,0:T(8,128)S(1)} %copy-done.18), channel_id=1, source_target_pairs={{0,1},{1,2},{2,3},{4,5},{5,6},{6,7},{8,9},{9,10},{10,11},{12,13},{... | collective-permute-start | bytes 442376 | tf_op jit(solution)/shard_map/ppermute | solution.py:27
  197.2 181.4 %copy-start.2 = (f32[3,24,16,128]{3,2,1,0:T(8,128)S(1)}, f32[3,24,16,128]{3,2,1,0:T(8,128)}, u32[]{:S(2)}) copy-start(f32[3,24,16,128]{3,2,1,0:T(8,128)} %copy-done.1) | copy-start | bytes 1769476
  372.4 8.6 %collective-permute-start.18 = (f32[8,32,160]{2,1,0:T(8,128)S(1)}, f32[8,32,160]{2,1,0:T(8,128)S(1)}, u32[]{:S(2)}, u32[]{:S(2)}) collective-permute-start(f32[8,32,160]{2,1,0:T(8,128)S(1)} %get-tuple-element.1053), channel_id=1, source_target_pairs={{0,16},{1,17},{2,18},{3,19},{4,20},{5,21},{6,22},{7,23},{8,24},{9,... | collective-permute-start | bytes 491528 | tf_op jit(solution)/shard_map/ppermute | solution.py:27
  377.1 8.3 %collective-permute-start.19 = (f32[8,32,160]{2,1,0:T(8,128)S(1)}, f32[8,32,160]{2,1,0:T(8,128)S(1)}, u32[]{:S(2)}, u32[]{:S(2)}) collective-permute-start(f32[8,32,160]{2,1,0:T(8,128)S(1)} %get-tuple-element.1054), channel_id=1, source_target_pairs={{16,0},{17,1},{18,2},{19,3},{20,4},{21,5},{22,6},{23,7},{24,8},{25... | collective-permute-start | bytes 491528 | tf_op jit(solution)/shard_map/ppermute | solution.py:28
  385.5 17.7 %collective-permute-start.20 = (f32[16,8,160]{2,1,0:T(8,128)S(1)}, f32[16,8,160]{2,1,0:T(8,128)S(1)}, u32[]{:S(2)}, u32[]{:S(2)}) collective-permute-start(f32[16,8,160]{2,1,0:T(8,128)S(1)} %get-tuple-element.1059), channel_id=1, source_target_pairs={{0,4},{4,8},{8,12},{1,5},{5,9},{9,13},{2,6},{6,10},{10,14},{3,7},{... | collective-permute-start | bytes 245768 | tf_op jit(solution)/shard_map/ppermute | solution.py:27
  393.4 9.8 %collective-permute-start.21 = (f32[16,8,160]{2,1,0:T(8,128)S(1)}, f32[16,8,160]{2,1,0:T(8,128)S(1)}, u32[]{:S(2)}, u32[]{:S(2)}) collective-permute-start(f32[16,8,160]{2,1,0:T(8,128)S(1)} %get-tuple-element.1060), channel_id=1, source_target_pairs={{4,0},{8,4},{12,8},{5,1},{9,5},{13,9},{6,2},{10,6},{14,10},{7,3},{... | collective-permute-start | bytes 245768 | tf_op jit(solution)/shard_map/ppermute | solution.py:28
  394.8 21.3 %collective-permute-start.3 = (f32[3,24,4,128]{3,1,2,0:T(8,128)S(1)}, f32[3,24,4,128]{3,1,2,0:T(8,128)S(1)}, u32[]{:S(2)}, u32[]{:S(2)}) collective-permute-start(f32[3,24,4,128]{3,1,2,0:T(8,128)S(1)} %copy.408), channel_id=1, source_target_pairs={{0,4},{4,8},{8,12},{1,5},{5,9},{9,13},{2,6},{6,10},{10,14},{3,7},{... | collective-permute-start | bytes 442376 | tf_op jit(solution)/shard_map/ppermute | solution.py:27
  401.9 10.9 %collective-permute-start.2 = (f32[3,24,4,128]{3,1,2,0:T(8,128)S(1)}, f32[3,24,4,128]{3,1,2,0:T(8,128)S(1)}, u32[]{:S(2)}, u32[]{:S(2)}) collective-permute-start(f32[3,24,4,128]{3,1,2,0:T(8,128)S(1)} %copy.407), channel_id=1, source_target_pairs={{4,0},{8,4},{12,8},{5,1},{9,5},{13,9},{6,2},{10,6},{14,10},{7,3},{... | collective-permute-start | bytes 442376 | tf_op jit(solution)/shard_map/ppermute | solution.py:28
  403.3 16.2 %collective-permute-start.22 = (f32[16,16,16]{2,1,0:T(8,128)S(1)}, f32[16,16,16]{2,1,0:T(8,128)S(1)}, u32[]{:S(2)}, u32[]{:S(2)}) collective-permute-start(f32[16,16,16]{2,1,0:T(8,128)S(1)} %get-tuple-element.1068), channel_id=1, source_target_pairs={{0,1},{1,2},{2,3},{4,5},{5,6},{6,7},{8,9},{9,10},{10,11},{12,13},{... | collective-permute-start | bytes 49160 | tf_op jit(solution)/shard_map/ppermute | solution.py:27
  407.8 11.7 %collective-permute-start.23 = (f32[16,16,16]{2,1,0:T(8,128)S(1)}, f32[16,16,16]{2,1,0:T(8,128)S(1)}, u32[]{:S(2)}, u32[]{:S(2)}) collective-permute-start(f32[16,16,16]{2,1,0:T(8,128)S(1)} %get-tuple-element.1069), channel_id=1, source_target_pairs={{1,0},{2,1},{3,2},{5,4},{6,5},{7,6},{9,8},{10,9},{11,10},{13,12},{... | collective-permute-start | bytes 49160 | tf_op jit(solution)/shard_map/ppermute | solution.py:28
  595.0 11.0 %collective-permute-start.24 = (f32[8,32,160]{2,1,0:T(8,128)S(1)}, f32[8,32,160]{2,1,0:T(8,128)S(1)}, u32[]{:S(2)}, u32[]{:S(2)}) collective-permute-start(f32[8,32,160]{2,1,0:T(8,128)S(1)} %get-tuple-element.1051), channel_id=1, source_target_pairs={{0,16},{1,17},{2,18},{3,19},{4,20},{5,21},{6,22},{7,23},{8,24},{9,... | collective-permute-start | bytes 491528 | tf_op jit(solution)/shard_map/ppermute | solution.py:27
  597.0 10.1 %collective-permute-start.25 = (f32[8,32,160]{2,1,0:T(8,128)S(1)}, f32[8,32,160]{2,1,0:T(8,128)S(1)}, u32[]{:S(2)}, u32[]{:S(2)}) collective-permute-start(f32[8,32,160]{2,1,0:T(8,128)S(1)} %get-tuple-element.1052), channel_id=1, source_target_pairs={{16,0},{17,1},{18,2},{19,3},{20,4},{21,5},{22,6},{23,7},{24,8},{25... | collective-permute-start | bytes 491528 | tf_op jit(solution)/shard_map/ppermute | solution.py:28
  607.3 11.9 %collective-permute-start.26 = (f32[16,8,160]{2,1,0:T(8,128)S(1)}, f32[16,8,160]{2,1,0:T(8,128)S(1)}, u32[]{:S(2)}, u32[]{:S(2)}) collective-permute-start(f32[16,8,160]{2,1,0:T(8,128)S(1)} %get-tuple-element.1057), channel_id=1, source_target_pairs={{0,4},{4,8},{8,12},{1,5},{5,9},{9,13},{2,6},{6,10},{10,14},{3,7},{... | collective-permute-start | bytes 245768 | tf_op jit(solution)/shard_map/ppermute | solution.py:27
  610.0 9.2 %collective-permute-start.27 = (f32[16,8,160]{2,1,0:T(8,128)S(1)}, f32[16,8,160]{2,1,0:T(8,128)S(1)}, u32[]{:S(2)}, u32[]{:S(2)}) collective-permute-start(f32[16,8,160]{2,1,0:T(8,128)S(1)} %get-tuple-element.1058), channel_id=1, source_target_pairs={{4,0},{8,4},{12,8},{5,1},{9,5},{13,9},{6,2},{10,6},{14,10},{7,3},{... | collective-permute-start | bytes 245768 | tf_op jit(solution)/shard_map/ppermute | solution.py:28
  611.9 20.7 %collective-permute-start.4 = (f32[3,24,24,4]{2,1,3,0:T(8,128)}, f32[3,24,24,4]{2,1,3,0:T(8,128)}, u32[]{:S(2)}, u32[]{:S(2)}) collective-permute-start(f32[3,24,24,4]{2,1,3,0:T(8,128)} %get-tuple-element.1045), channel_id=1, source_target_pairs={{1,0},{2,1},{3,2},{5,4},{6,5},{7,6},{9,8},{10,9},{11,10},{13,12},{... | collective-permute-start | bytes 82952 | tf_op jit(solution)/shard_map/ppermute | solution.py:28
  613.2 18.0 %collective-permute-start.5 = (f32[3,24,24,4]{2,1,3,0:T(8,128)S(1)}, f32[3,24,24,4]{2,1,3,0:T(8,128)}, u32[]{:S(2)}, u32[]{:S(2)}) collective-permute-start(f32[3,24,24,4]{2,1,3,0:T(8,128)S(1)} %get-tuple-element.1046), channel_id=1, source_target_pairs={{0,1},{1,2},{2,3},{4,5},{5,6},{6,7},{8,9},{9,10},{10,11},{12,13},{... | collective-permute-start | bytes 82952 | tf_op jit(solution)/shard_map/ppermute | solution.py:27
  620.0 15.0 %collective-permute-start.28 = (f32[16,16,16]{2,1,0:T(8,128)}, f32[16,16,16]{2,1,0:T(8,128)}, u32[]{:S(2)}, u32[]{:S(2)}) collective-permute-start(f32[16,16,16]{2,1,0:T(8,128)} %get-tuple-element.1066), channel_id=1, source_target_pairs={{0,1},{1,2},{2,3},{4,5},{5,6},{6,7},{8,9},{9,10},{10,11},{12,13},{... | collective-permute-start | bytes 49160 | tf_op jit(solution)/shard_map/ppermute | solution.py:27
  623.9 11.1 %collective-permute-start.29 = (f32[16,16,16]{2,1,0:T(8,128)}, f32[16,16,16]{2,1,0:T(8,128)}, u32[]{:S(2)}, u32[]{:S(2)}) collective-permute-start(f32[16,16,16]{2,1,0:T(8,128)} %get-tuple-element.1067), channel_id=1, source_target_pairs={{1,0},{2,1},{3,2},{5,4},{6,5},{7,6},{9,8},{10,9},{11,10},{13,12},{... | collective-permute-start | bytes 49160 | tf_op jit(solution)/shard_map/ppermute | solution.py:28
  (44 other events, 316.1 us)
where the time goes:
time: 651 us; the launch traced here: 642 us
  local copies, waits for them, and re-layouts  300 us (46%)
  other arithmetic  154 us (24%)
  starting transfers between devices  91.3 us (14%)
  loops' own time  78.1 us (12%)
  waiting for transfers between devices  17.4 us (3%)
    dynamic_update_slice x32, local copies, waits for them, and re-layouts, add_block(): lax.dynamic_update_slice(accumulated, current + weight_z[a] * along_y, co...  124 us
    add x32, other arithmetic, add_block(): current + weight_z[a] * along_y  102 us
    gather x96, local copies, waits for them, and re-layouts  102 us
    another operation x2, loops' own time, spread_blocks(): return lax.fori_loop(0, values.shape[0], add_block, accumulated)  77.6 us
    ppermute x15, starting transfers between devices, with_halo(): before = lax.ppermute(last, axis, up)  71.8 us
    add x8, other arithmetic, add_block(): sum((weight_x[a] * jnp.pad(block_vals, ((a, 3 - a), (0, 0), (0, 0))) for...  20.5 us
    ppermute x15, starting transfers between devices, with_halo(): after = lax.ppermute(initial, axis, down)  19.5 us
    dynamic_slice x24, local copies, waits for them, and re-layouts, add_block(): corner = (start_x[b], start_y[b], start_z[b] + a)  14.4 us
  transfers between devices with their start and end apart: 30, of which 10 were waited for; matrix products, arithmetic and copies ran while one was open for 47% of the time, Pallas kernels for 0%

commit v1 on v0

v1 whole, which is shorter than its diff:
```python
import functools

import jax
import jax.numpy as jnp
from jax import lax
from jax.experimental import pallas as pl
from jax.experimental.pallas import tpu as pltpu
from jax.sharding import PartitionSpec as P

BX = 8
BY = 8
BZ = 128
RX = 6
RY = 6
RZ = 14
STEPS = 2

STEP_SIZE = 0.5
REG_WEIGHT = 0.1
LAPLACE_TAPS = (-205.0 / 72.0, 8.0 / 5.0, -1.0 / 5.0, 8.0 / 315.0, -1.0 / 560.0)

HX = RX + 2
HY = RY + 2
HZ = RZ + 2
LANES = 128
WIDE = 2 * HZ
PK = LANES // WIDE
XG = HX // PK
LH = 4
VPK = LANES // (2 * LH)
WX = BX + 2 * HX
WY = BY + 2 * HY
MESH = pl.DeviceIdType.MESH


def kernel(shape, vel, grad, shx, shy, shz, frac, out,
           E0, E1, U, T, YP, XP, ACC0, ACC1, BU, ST, ADJ,
           S, RZD, RZU, YRD, YRU, XPD, XPU, XMD, XMU, ZS, ZRD, ZRU,
           VE, YSU, YSD, YVD, YVU, SV, VRD, VRU, send, recv):
    TX, TY, TZ = vel.shape[1:]
    NBX, NBY = TX // BX, TY // BY
    EX = TX + 2 * HX
    EG = EX // PK
    G = TX // PK
    OX = slice(HX, HX + TX)
    OY = slice(HY, HY + TY)
    OP = slice(EX + XG, EX + XG + G)

    at = {a: lax.axis_index(a) for a in shape}
    up = {a: at[a] < shape[a] - 1 for a in shape}
    dn = {a: at[a] > 0 for a in shape}

    sends = []
    count = [0]

    class Copy:
        def __init__(self, src, dst, axis, way, also=None):
            i = count[0]
            count[0] += 1
            to = at[axis] + way
            self.desc = pltpu.make_async_remote_copy(
                src_ref=src, dst_ref=dst, send_sem=send.at[i], recv_sem=recv.at[i],
                device_id={axis: to}, device_id_type=MESH)
            self.out = up[axis] if way > 0 else dn[axis]
            self.into = dn[axis] if way > 0 else up[axis]
            if also is not None:
                self.out = jnp.logical_and(self.out, also)
                self.into = jnp.logical_and(self.into, also)
            sends.append(self)

        def start(self):
            @pl.when(self.out)
            def _():
                self.desc.start()
            return self

        def landed(self):
            @pl.when(self.into)
            def _():
                self.desc.wait_recv()

        def left(self):
            @pl.when(self.out)
            def _():
                self.desc.wait_send()

    lane = lax.broadcasted_iota(jnp.int32, (1, 1, LANES), 2)
    lane2 = lax.broadcasted_iota(jnp.int32, (1, LANES), 1)

    for ref in (E0, E1, YP, XP, ACC0, ACC1, BU, RZD, RZU, YRD, YRU, XPD, XPU, XMD, XMU,
                ZRD, ZRU, VE, YVD, YVU, VRD, VRU):
        ref[...] = jnp.zeros_like(ref)

    barrier = pltpu.get_barrier_semaphore()
    total = jnp.int32(0)
    for a in shape:
        for way, has in ((1, up[a]), (-1, dn[a])):
            @pl.when(has)
            def _(a=a, way=way):
                pl.semaphore_signal(barrier, inc=1, device_id={a: at[a] + way}, device_id_type=MESH)
            total = total + has.astype(jnp.int32)
    pl.semaphore_wait(barrier, total)

    def pack_own(E):
        for g in range(G):
            row = None
            for j in range(PK):
                turned = pltpu.roll(E[HX + PK * g + j, OY, :], (WIDE * j + HZ) % LANES, 1)
                row = turned if row is None else jnp.where(lane2 // WIDE == j, turned, row)
            S_of(E)[g] = row

    def S_of(E):
        return S.at[0] if E is E0 else S.at[1]

    def forward_exchange(E, k, between):
        s, rd, ru = S.at[k], RZD.at[k], RZU.at[k]
        zu = Copy(s, rd, "gz", 1).start()
        zd = Copy(s, ru, "gz", -1).start()
        lo_x, hi_x = slice(0, HX), slice(HX + TX, EX)
        xmu = Copy(E.at[TX:TX + HX, OY, :], E.at[lo_x, OY, :], "gx", 1).start()
        xmd = Copy(E.at[HX:2 * HX, OY, :], E.at[hi_x, OY, :], "gx", -1).start()
        top, bottom = slice(TY, TY + HY), slice(HY, 2 * HY)
        below, above = slice(0, HY), slice(HY + TY, 2 * HY + TY)

        def to_y(layers, also=None):
            return [Copy(E.at[layers, top, :], E.at[layers, below, :], "gy", 1, also).start(),
                    Copy(E.at[layers, bottom, :], E.at[layers, above, :], "gy", -1, also).start()]

        ys = to_y(OX)
        between()
        zu.landed()
        zd.landed()
        E[OP, OY, :] = jnp.where(lane % WIDE < HZ, rd[...], ru[...])
        first_p, last_p = slice(EX + XG, EX + 2 * XG), slice(EX + G, EX + G + XG)
        lo_p, hi_p = slice(EX, EX + XG), slice(EX + XG + G, EX + EG)
        xpu = Copy(E.at[last_p, OY, :], E.at[lo_p, OY, :], "gx", 1).start()
        xpd = Copy(E.at[first_p, OY, :], E.at[hi_p, OY, :], "gx", -1).start()
        ys += to_y(OP)
        xmu.landed()
        ys += to_y(lo_x, dn["gx"])
        xmd.landed()
        ys += to_y(hi_x, up["gx"])
        xpu.landed()
        ys += to_y(lo_p, dn["gx"])
        xpd.landed()
        ys += to_y(hi_p, up["gx"])
        for y in ys:
            y.landed()

    def unpack(E):
        for g in range(EG):
            row = E[EX + g]
            for j in range(PK):
                U[PK * g + j] = pltpu.roll(row, (LANES - (WIDE * j + HZ)) % LANES, 1)

    def taps(k, d, bx, by):
        e = frac[k, d, bx, by, 0].astype(jnp.float32) * 0.125
        e2 = e * e
        e3 = e2 * e
        return (0.5 * (2.0 * e2 - e3 - e), 0.5 * (3.0 * e3 - 5.0 * e2 + 2.0),
                0.5 * (4.0 * e2 - 3.0 * e3 + e), 0.5 * (e3 - e2))

    def gather_block(E, k, bx, by):
        a, b, c = shx[k, bx, by, 0], shy[k, bx, by, 0], shz[k, bx, by, 0]
        wx, wy, wz = (taps(k, d, bx, by) for d in range(3))
        y0 = by * BY if isinstance(by, int) else pl.multiple_of(by * BY, BY)
        x0 = bx * BX + (a + HX - 1)
        for i, ref in enumerate((E, U)):
            win = ref[pl.ds(x0, BX + 3), pl.ds(y0, WY), :]
            T[i * BX:(i + 1) * BX] = sum(wx[u] * win[u:u + BX] for u in range(4))
        y = sum(wy[v] * T[:, pl.ds(b + (HY - 1 + v), BY), :] for v in range(4))
        own, rim = y[:BX].reshape(BX * BY, LANES), y[BX:].reshape(BX * BY, LANES)
        res = None
        for w in range(4):
            s = c + (w - 1)
            inside = jnp.logical_and(lane2 >= s, lane2 < LANES + s)
            term = wz[w] * pltpu.roll(jnp.where(inside, own, rim), lax.rem(LANES - s, LANES), 1)
            res = term if res is None else res + term
        return res.reshape(BX, BY, LANES)

    def spread_block(ACC, vals, k, bx, by):
        a, b, c = shx[k, bx, by, 0], shy[k, bx, by, 0], shz[k, bx, by, 0]
        wx, wy, wz = (taps(k, d, bx, by) for d in range(3))
        flat = vals.reshape(BX * BY, LANES)
        own = rim = None
        for w in range(4):
            s = c + (w - 1)
            inside = jnp.logical_and(lane2 >= s, lane2 < LANES + s)
            term = wz[w] * pltpu.roll(flat, lax.rem(LANES + s, LANES), 1)
            o, r = jnp.where(inside, term, 0.0), jnp.where(inside, 0.0, term)
            own, rim = (o, r) if own is None else (own + o, rim + r)
        YP[0:BX, 2 * HY:2 * HY + BY, :] = own.reshape(BX, BY, LANES)
        YP[BX:2 * BX, 2 * HY:2 * HY + BY, :] = rim.reshape(BX, BY, LANES)
        t = sum(wy[v] * YP[:, pl.ds((HY + 1 - v) - b, WY), :] for v in range(4))
        y0 = by * BY if isinstance(by, int) else pl.multiple_of(by * BY, BY)
        x0 = bx * BX
        for i, ref in enumerate((ACC, BU)):
            for m in range(BX + 3):
                XP[i, 2 * HX + m] = sum(wx[u] * t[i * BX + m - u] for u in range(4) if 0 <= m - u < BX)
            here = (pl.ds(x0, WX), pl.ds(y0, WY), slice(None))
            ref[here] = ref[here] + XP[i, pl.ds((HX + 1) - a, WX)]

    def pack_rims(ACC):
        for g in range(EG):
            ACC[EX + g] = sum(pltpu.roll(BU[PK * g + j], (WIDE * j + HZ) % LANES, 1) for j in range(PK))

    def return_exchange(ACC, k, between):
        yrd, yru = YRD.at[k], YRU.at[k]
        below, above = slice(0, HY), slice(HY + TY, 2 * HY + TY)
        top, bottom = slice(TY, TY + HY), slice(HY, 2 * HY)

        def to_y(layers, also=None):
            return (Copy(ACC.at[layers, above, :], yrd.at[layers], "gy", 1, also).start(),
                    Copy(ACC.at[layers, below, :], yru.at[layers], "gy", -1, also).start())

        def fold_y(copies, layers):
            copies[0].landed()
            copies[1].landed()
            ACC[layers, bottom, :] = ACC[layers, bottom, :] + yrd[layers]
            ACC[layers, top, :] = ACC[layers, top, :] + yru[layers]

        lo_p, hi_p = slice(EX, EX + XG), slice(EX + XG + G, EX + EG)
        lo_x, hi_x = slice(0, HX), slice(HX + TX, EX)
        ylp = to_y(lo_p, dn["gx"])
        yhp = to_y(hi_p, up["gx"])
        ylx = to_y(lo_x, dn["gx"])
        yhx = to_y(hi_x, up["gx"])
        yop = to_y(OP)
        yom = to_y(OX)
        between()
        fold_y(ylp, lo_p)
        xpd = Copy(ACC.at[lo_p, OY, :], XPU.at[k], "gx", -1).start()
        fold_y(yhp, hi_p)
        xpu = Copy(ACC.at[hi_p, OY, :], XPD.at[k], "gx", 1).start()
        fold_y(ylx, lo_x)
        xmd = Copy(ACC.at[lo_x, OY, :], XMU.at[k], "gx", -1).start()
        fold_y(yhx, hi_x)
        xmu = Copy(ACC.at[hi_x, OY, :], XMD.at[k], "gx", 1).start()
        fold_y(yop, OP)
        xpd.landed()
        xpu.landed()
        first_p, last_p = slice(EX + XG, EX + 2 * XG), slice(EX + G, EX + G + XG)
        ACC[first_p, OY, :] = ACC[first_p, OY, :] + XPD[k]
        ACC[last_p, OY, :] = ACC[last_p, OY, :] + XPU[k]
        ZS[k] = ACC[OP, OY, :]
        zu = Copy(ZS.at[k], ZRD.at[k], "gz", 1).start()
        zd = Copy(ZS.at[k], ZRU.at[k], "gz", -1).start()
        fold_y(yom, OX)
        xmd.landed()
        xmu.landed()
        ACC[HX:2 * HX, OY, :] = ACC[HX:2 * HX, OY, :] + XMD[k]
        ACC[TX:TX + HX, OY, :] = ACC[TX:TX + HX, OY, :] + XMU[k]
        zu.landed()
        zd.landed()
        rims = jnp.where(lane % WIDE >= HZ, ZRD[k], ZRU[k])
        edge = jnp.logical_or(lane2 < HZ, lane2 >= LANES - HZ)
        for g in range(G):
            for j in range(PK):
                x = PK * g + j
                turned = pltpu.roll(rims[g], (LANES - (WIDE * j + HZ)) % LANES, 1)
                ADJ[x] = ACC[HX + x, OY, :] + jnp.where(edge, turned, 0.0)

    def each_block(fn):
        def step(n, carry):
            fn(n // NBY, n % NBY)
            return carry
        lax.fori_loop(0, NBX * NBY, step, 0)

    g0 = sum(grad[0, c].astype(jnp.float32) * vel[c] for c in range(3))
    E0[OX, OY, :] = STEP_SIZE * g0
    pack_own(E0)

    def nothing():
        pass

    forward_exchange(E0, 0, nothing)

    faces = []

    def send_faces():
        VE[:, LH:LH + TX, OY, :] = vel[...]
        for c in range(3):
            for i in range(TX // 2):
                for h in range(2):
                    YSU[c, i, LH * h:LH * (h + 1), :] = vel[c, 2 * i + h, TY - LH:TY, :]
                    YSD[c, i, LH * h:LH * (h + 1), :] = vel[c, 2 * i + h, 0:LH, :]
            for g in range(TX // VPK):
                row = None
                for j in range(VPK):
                    turned = pltpu.roll(vel[c, VPK * g + j], (2 * LH * j + LH) % LANES, 1)
                    row = turned if row is None else jnp.where(lane2 // (2 * LH) == j, turned, row)
                SV[c, g] = row
        faces.extend([
            Copy(SV, VRD, "gz", 1).start(), Copy(SV, VRU, "gz", -1).start(),
            Copy(vel.at[:, TX - LH:TX], VE.at[:, 0:LH, OY, :], "gx", 1).start(),
            Copy(vel.at[:, 0:LH], VE.at[:, LH + TX:2 * LH + TX, OY, :], "gx", -1).start(),
            Copy(YSU, YVD, "gy", 1).start(), Copy(YSD, YVU, "gy", -1).start()])

    send_faces()
    unpack(E0)

    def first(bx, by):
        y0 = pl.multiple_of(by * BY, BY)
        ST[pl.ds(bx * BX, BX), pl.ds(y0, BY), :] = gather_block(E0, 0, bx, by)

    each_block(first)
    g1 = sum(grad[1, c].astype(jnp.float32) * vel[c] for c in range(3))
    E1[OX, OY, :] = ST[...] + STEP_SIZE * g1
    pack_own(E1)

    forward_exchange(E1, 1, nothing)
    unpack(E1)

    def second(bx, by):
        spread_block(ACC1, gather_block(E1, 1, bx, by), 1, bx, by)

    each_block(second)
    pack_rims(ACC1)

    def regular():
        for f in faces:
            f.landed()
        for c in range(3):
            for i in range(TX // 2):
                for h in range(2):
                    VE[c, LH + 2 * i + h, HY - LH:HY, :] = YVD[c, i, LH * h:LH * (h + 1), :]
                    VE[c, LH + 2 * i + h, HY + TY:HY + TY + LH, :] = YVU[c, i, LH * h:LH * (h + 1), :]
        rows = lax.broadcasted_iota(jnp.int32, (2 * LANES, LANES), 0)
        cols = lax.broadcasted_iota(jnp.int32, (2 * LANES, LANES), 1)
        r = rows - LANES
        place = jnp.where(rows < LANES, rows, jnp.where(r < LH, r + LANES, r - LANES))
        known = jnp.logical_or(rows < LANES, jnp.logical_or(r < LH, r >= LANES - LH))
        gap = jnp.abs(place - cols)
        band = jnp.zeros((2 * LANES, LANES), jnp.float32)
        for k in range(5):
            tap = (3.0 if k == 0 else 1.0) * LAPLACE_TAPS[k]
            band = jnp.where(jnp.logical_and(known, gap == k), tap, band)
        for c in range(3):
            rims = []
            for g in range(TX // VPK):
                row = jnp.where(lane2 % (2 * LH) < LH, VRD[c, g], VRU[c, g])
                for j in range(VPK):
                    rims.append(pltpu.roll(row, (LANES - (2 * LH * j + LH)) % LANES, 1))
            rim = jnp.concatenate(rims, axis=0)
            own = vel[c].reshape(TX * TY, LANES)
            res = jnp.dot(jnp.concatenate([own, rim], axis=1), band,
                          preferred_element_type=jnp.float32,
                          precision=lax.Precision.HIGHEST).reshape(TX, TY, LANES)
            for k in range(1, 5):
                res = res + LAPLACE_TAPS[k] * (
                    VE[c, LH + k:LH + k + TX, OY, :] + VE[c, LH - k:LH - k + TX, OY, :]
                    + VE[c, LH:LH + TX, HY + k:HY + k + TY, :]
                    + VE[c, LH:LH + TX, HY - k:HY - k + TY, :])
            out[c] = (-REG_WEIGHT) * res

    return_exchange(ACC1, 1, regular)

    def third(bx, by):
        y0 = pl.multiple_of(by * BY, BY)
        vals = ADJ[pl.ds(bx * BX, BX), pl.ds(y0, BY), :]
        spread_block(ACC0, vals, 0, bx, by)

    BU[...] = jnp.zeros_like(BU)
    each_block(third)
    pack_rims(ACC0)

    def add_gauss(k):
        for c in range(3):
            out[c] = out[c] + STEP_SIZE * grad[k, c].astype(jnp.float32) * ADJ[...]

    return_exchange(ACC0, 0, functools.partial(add_gauss, 1))
    add_gauss(0)
    for copy in sends:
        copy.left()


COPIES = 18 * 2 + 18 * 2 + 6


def body(shape, velocity, gradients, shift_x, shift_y, shift_z, fractions):
    TX, TY, TZ = velocity.shape[1:]
    assert TZ == BZ == LANES and TX % VPK == 0 and TX % BX == 0 and TY % BY == 0
    EX, EY = TX + 2 * HX, TY + 2 * HY
    EG, G = EX // PK, TX // PK
    vm = lambda *s: pltpu.VMEM(s, jnp.float32)
    vmem = pl.BlockSpec(memory_space=pltpu.VMEM)
    smem = pl.BlockSpec(memory_space=pltpu.SMEM)
    return pl.pallas_call(
        functools.partial(kernel, shape),
        out_shape=jax.ShapeDtypeStruct(velocity.shape, jnp.float32),
        in_specs=[vmem, vmem, smem, smem, smem, smem],
        out_specs=vmem,
        scratch_shapes=[
            vm(EX + EG, EY, LANES), vm(EX + EG, EY, LANES),
            vm(EX, EY, LANES), vm(2 * BX, WY, LANES),
            vm(2 * BX, 2 * WY - BY, LANES), vm(2, 2 * WX - BX, WY, LANES),
            vm(EX + EG, EY, LANES), vm(EX + EG, EY, LANES),
            vm(EX, EY, LANES), vm(TX, TY, LANES), vm(TX, TY, LANES),
            vm(2, G, TY, LANES), vm(2, G, TY, LANES), vm(2, G, TY, LANES),
            vm(2, EX + EG, HY, LANES), vm(2, EX + EG, HY, LANES),
            vm(2, XG, TY, LANES), vm(2, XG, TY, LANES),
            vm(2, HX, TY, LANES), vm(2, HX, TY, LANES),
            vm(2, G, TY, LANES), vm(2, G, TY, LANES), vm(2, G, TY, LANES),
            vm(3, TX + 2 * LH, EY, LANES),
            vm(3, TX // 2, 2 * LH, LANES), vm(3, TX // 2, 2 * LH, LANES),
            vm(3, TX // 2, 2 * LH, LANES), vm(3, TX // 2, 2 * LH, LANES),
            vm(3, TX // VPK, TY, LANES), vm(3, TX // VPK, TY, LANES), vm(3, TX // VPK, TY, LANES),
            pltpu.SemaphoreType.DMA((COPIES,)), pltpu.SemaphoreType.DMA((COPIES,)),
        ],
        compiler_params=pltpu.CompilerParams(collective_id=0, has_side_effects=True),
    )(velocity, gradients, shift_x, shift_y, shift_z, fractions)


def solution(mesh):
    in_specs = (
        P(None, "gx", "gy", "gz"),
        P(None, None, "gx", "gy", "gz"),
        P(None, "gx", "gy", "gz"),
        P(None, "gx", "gy", "gz"),
        P(None, "gx", "gy", "gz"),
        P(None, None, "gx", "gy", "gz"),
    )
    out_specs = P(None, "gx", "gy", "gz")
    return jax.shard_map(functools.partial(body, dict(mesh.shape)), mesh=mesh, in_specs=in_specs,
                         out_specs=out_specs, check_vma=False)
```

time: 651 us -> 46.7 us (0.07); the launches traced: 642 us -> 45.8 us
  local copies, waits for them, and re-layouts: 300 us -> 5.27 us
  other arithmetic: 154 us -> 0 us
  starting transfers between devices: 91.3 us -> 0 us
  loops' own time: 78.1 us -> 0 us
  Pallas kernels: 0 us -> 40.5 us
  waiting for transfers between devices: 17.4 us -> 0 us
    add x55 -> x0, other arithmetic: 134 us -> none  [the longest x32 102 us: add_block(): current + weight_z[a] * along_y]
    dynamic_update_slice x32 -> x0, local copies, waits for them, and re-layouts: 124 us -> none  [add_block(): lax.dynamic_update_slice(accumulated, current + weight_z[a] * along_y, co...]
    gather x96 -> x0, local copies, waits for them, and re-layouts: 102 us -> none
    ppermute x30 -> x0, starting transfers between devices: 91.3 us -> none  [the longest x15 71.8 us: with_halo(): before = lax.ppermute(last, axis, up)]
    another operation x10 -> x0, loops' own time: 78.1 us -> none  [the longest x2 77.6 us: spread_blocks(): return lax.fori_loop(0, values.shape[0], add_block, accumulated)]
    pallas_call x0 -> x1, Pallas kernels: none -> 40.5 us  [body(): pl.pallas_call(functools.partial(kernel, shape), out_shape=jax.ShapeDtype...]
    slice x42 -> x0, local copies, waits for them, and re-layouts: 18.8 us -> none  [the longest x8 5.39 us: add_block(): weight_z[a] * along_y]
    ppermute x30 -> x0, waiting for transfers between devices: 17.4 us -> none  [the longest x15 11.6 us: with_halo(): before = lax.ppermute(last, axis, up)]
  transfers between devices with their start and end apart: 30 -> 0, of which waited for: 10 -> 0; matrix products, arithmetic and copies ran while one was open for 47% -> 0% of each run, Pallas kernels for 0% -> 0%
where the time goes in v1:
time: 46.7 us; the launch traced here: 45.8 us
  Pallas kernels  40.5 us (87%)
  local copies, waits for them, and re-layouts  5.27 us (11%)
    pallas_call x1, Pallas kernels, body(): pl.pallas_call(functools.partial(kernel, shape), out_shape=jax.ShapeDtype...  40.5 us
    unnamed x11, local copies, waits for them, and re-layouts  5.27 us

profile of v1, /device:TPU:0, one launch (start us, length us, event | category | flops | bytes accessed | tf_op | source)
XLA Modules:
  0.0 45.8 jit_solution(5150945785032517423)
XLA Ops:
  0.0 0.0 copy-start.1
  0.0 1.4 %copy.7.shx = s32[2,2,2,1]{3,2,1,0:T(2,128)} copy(s32[2,2,2,1]{2,3,1,0:T(1,128)} %param.8) | data formatting | bytes 64 | tf_op args[2]
  1.4 0.0 copy-done.1
  1.4 0.0 copy-start.2
  1.4 0.7 %copy.8.shy = s32[2,2,2,1]{3,2,1,0:T(2,128)} copy(s32[2,2,2,1]{2,3,1,0:T(1,128)S(1)} %copy-done.1) | data formatting | bytes 64 | tf_op args[3]
  2.1 0.0 copy-done.2
  2.1 0.0 copy-start
  2.1 0.7 %copy.9.shz = s32[2,2,2,1]{3,2,1,0:T(2,128)} copy(s32[2,2,2,1]{2,3,1,0:T(1,128)S(1)} %copy-done.2) | data formatting | bytes 64 | tf_op args[4]
  2.8 0.0 copy-done
  2.8 0.7 %copy.10.frac = s32[2,3,2,2,1]{4,3,2,1,0:T(2,128)} copy(s32[2,3,2,2,1]{1,4,3,2,0:T(1,128)S(1)} %copy-done) | data formatting | bytes 192 | tf_op args[5]
  3.5 40.5 %shard_map.64 = f32[3,16,16,128]{3,2,1,0:T(8,128)} custom-call(f32[3,16,16,128]{3,2,1,0:T(8,128)} %vel.1, bf16[2,3,16,16,128]{4,3,2,1,0:T(8,128)(2,1)} %grad.1, s32[2,2,2,1]{3,2,1,0:T(2,128)} %copy.7.shx, s32[2,2,2,1]{3,2,1,0:T(2,128)} %copy.8.shy, s32[2,2,2,1]{3,2,1,0:T(2,128)} %copy.9.shz, s32[2,3,2,2,1]{4,3,2,1,0:T(2,128)} %copy.10.frac), custom_call_target="tpu_custom_call" | custom-call | tf_op jit(solution)/shard_map/pallas_call | solution.py:388
  44.0 1.8 %copy.12 = f32[3,16,16,128]{3,2,1,0:T(8,128)} copy(f32[3,16,16,128]{3,2,1,0:T(8,128)} %shard_map.64) | data formatting | bytes 786432
Async XLA Ops:
  0.0 1.4 %copy-start.1 = (s32[2,2,2,1]{2,3,1,0:T(1,128)S(1)}, s32[2,2,2,1]{2,3,1,0:T(1,128)}, u32[]{:S(2)}) copy-start(s32[2,2,2,1]{2,3,1,0:T(1,128)} %param.9) | copy-start | bytes 100
  1.4 0.7 %copy-start.2 = (s32[2,2,2,1]{2,3,1,0:T(1,128)S(1)}, s32[2,2,2,1]{2,3,1,0:T(1,128)}, u32[]{:S(2)}) copy-start(s32[2,2,2,1]{2,3,1,0:T(1,128)} %param.10) | copy-start | bytes 100
  2.1 0.7 %copy-start = (s32[2,3,2,2,1]{1,4,3,2,0:T(1,128)S(1)}, s32[2,3,2,2,1]{1,4,3,2,0:T(1,128)}, u32[]{:S(2)}) copy-start(s32[2,3,2,2,1]{1,4,3,2,0:T(1,128)} %param.11) | copy-start | bytes 292

commit v2 on v1

v2 whole, which is shorter than its diff:
```python
import functools

import jax
import jax.numpy as jnp
from jax import lax
from jax.experimental import pallas as pl
from jax.experimental.pallas import tpu as pltpu
from jax.sharding import PartitionSpec as P

BX = 8
BY = 8
BZ = 128
RX = 6
RY = 6
RZ = 14
STEPS = 2

STEP_SIZE = 0.5
REG_WEIGHT = 0.1
LAPLACE_TAPS = (-205.0 / 72.0, 8.0 / 5.0, -1.0 / 5.0, 8.0 / 315.0, -1.0 / 560.0)

HX = RX + 2
HY = RY + 2
HZ = RZ + 2
LANES = 128
PK = LANES // HZ
XG = HX // PK
LH = 4
VPK = LANES // (2 * LH)
WX = BX + 2 * HX
WY = BY + 2 * HY
MESH = pl.DeviceIdType.MESH
AXES = ("gx", "gy", "gz")
WAYS = sorted(((i, j, k) for i in (-1, 0, 1) for j in (-1, 0, 1) for k in (-1, 0, 1) if (i, j, k) != (0, 0, 0)),
              key=lambda d: -sum(map(abs, d)))


def piece(way, own, halo):
    return {-1: (0, halo), 0: (halo, halo + own), 1: (halo + own, 2 * halo + own)}[way]


def border(way, own, halo):
    return {-1: (halo, 2 * halo), 0: (halo, halo + own), 1: (own, halo + own)}[way]


def kernel(shape, vel, grad, shx, shy, shz, frac, out,
           E0, E1, U, T, YP, XP, ACC0, ACC1, BU, ST, ADJ, SP, SUM,
           VE, YSU, YSD, YVD, YVU, SV, VRD, VRU, *rest):
    back, (send, recv) = rest[:-2], rest[-2:]
    TX, TY, TZ = vel.shape[1:]
    NBX, NBY = TX // BX, TY // BY
    EX = TX + 2 * HX
    EG = EX // PK
    G = TX // PK
    OX = slice(HX, HX + TX)
    OY = slice(HY, HY + TY)

    at = {a: lax.axis_index(a) for a in AXES}

    def has(way):
        ok = None
        for a, w in zip(AXES, way):
            if w:
                one = at[a] < shape[a] - 1 if w > 0 else at[a] > 0
                ok = one if ok is None else jnp.logical_and(ok, one)
        return ok

    def device(way):
        return {a: at[a] + w for a, w in zip(AXES, way) if w}

    sends = []

    class Copy:
        def __init__(self, src, dst, way):
            i = len(sends)
            self.desc = pltpu.make_async_remote_copy(
                src_ref=src, dst_ref=dst, send_sem=send.at[i], recv_sem=recv.at[i],
                device_id=device(way), device_id_type=MESH)
            self.out, self.into = has(way), has(tuple(-w for w in way))
            sends.append(self)

        def start(self):
            pl.when(self.out)(self.desc.start)
            return self

        def landed(self):
            pl.when(self.into)(self.desc.wait_recv)

        def left(self):
            pl.when(self.out)(self.desc.wait_send)

    lane = lax.broadcasted_iota(jnp.int32, (1, 1, LANES), 2)
    lane2 = lax.broadcasted_iota(jnp.int32, (1, LANES), 1)

    for ref in (E0, E1, VE, YVD, YVU, VRD, VRU) + tuple(back):
        ref[...] = jnp.zeros_like(ref)

    barrier = pltpu.get_barrier_semaphore()
    total = jnp.int32(0)
    for way in WAYS:
        @pl.when(has(way))
        def _(way=way):
            pl.semaphore_signal(barrier, inc=1, device_id=device(way), device_id_type=MESH)
        total = total + has(way).astype(jnp.int32)

    def pack_own(E, k):
        for g in range(G):
            for side in range(2):
                row = None
                for j in range(PK):
                    turned = pltpu.roll(E[HX + PK * g + j, OY, :], (HZ * j + HZ * side) % LANES, 1)
                    row = turned if row is None else jnp.where(lane2 // HZ == j, turned, row)
                SP[k, side, HX // PK + g, OY, :] = row

    def region(way, dim_of):
        (x0, x1) = dim_of(way[0], G if way[2] else TX, XG if way[2] else HX)
        (y0, y1) = dim_of(way[1], TY, HY)
        return slice(x0, x1), slice(y0, y1)

    def rim(ref, way, where):
        xs, ys = where
        base = {0: 0, -1: EX, 1: EX + EG}[way]
        return ref.at[slice(base + xs.start, base + xs.stop), ys, :]

    def forward_exchange(E, k, between):
        copies = []
        for way in WAYS:
            xs, ys = region(way, border)
            if way[2]:
                src = SP.at[k, 0 if way[2] < 0 else 1, xs, ys, :]
            else:
                src = E.at[xs, ys, :]
            other = tuple(-w for w in way)
            copies.append(Copy(src, rim(E, other[2], region(other, piece)), way).start())
        between()
        for copy in copies:
            copy.landed()

    def unpack(E):
        for g in range(EG):
            below, above = E[EX + g], E[EX + EG + g]
            for j in range(PK):
                U[PK * g + j] = jnp.where(
                    lane2 < HZ, pltpu.roll(above, (LANES - HZ * j) % LANES, 1),
                    pltpu.roll(below, (LANES - HZ - HZ * j) % LANES, 1))

    def taps(k, d, bx, by):
        e = frac[k, bx, by, 0, d].astype(jnp.float32) * 0.125
        e2 = e * e
        e3 = e2 * e
        return (0.5 * (2.0 * e2 - e3 - e), 0.5 * (3.0 * e3 - 5.0 * e2 + 2.0),
                0.5 * (4.0 * e2 - 3.0 * e3 + e), 0.5 * (e3 - e2))

    def gather_block(E, k, bx, by):
        a, b, c = shx[k, bx, 0, by], shy[k, bx, 0, by], shz[k, bx, 0, by]
        wx, wy, wz = (taps(k, d, bx, by) for d in range(3))
        y0 = by * BY if isinstance(by, int) else pl.multiple_of(by * BY, BY)
        x0 = bx * BX + (a + HX - 1)
        for i, ref in enumerate((E, U)):
            win = ref[pl.ds(x0, BX + 3), pl.ds(y0, WY), :]
            T[i * BX:(i + 1) * BX] = sum(wx[u] * win[u:u + BX] for u in range(4))
        y = sum(wy[v] * T[:, pl.ds(b + (HY - 1 + v), BY), :] for v in range(4))
        own, rim = y[:BX].reshape(BX * BY, LANES), y[BX:].reshape(BX * BY, LANES)
        res = None
        for w in range(4):
            s = c + (w - 1)
            inside = jnp.logical_and(lane2 >= s, lane2 < LANES + s)
            term = wz[w] * pltpu.roll(jnp.where(inside, own, rim), lax.rem(LANES - s, LANES), 1)
            res = term if res is None else res + term
        return res.reshape(BX, BY, LANES)

    def spread_block(ACC, vals, k, bx, by):
        a, b, c = shx[k, bx, 0, by], shy[k, bx, 0, by], shz[k, bx, 0, by]
        wx, wy, wz = (taps(k, d, bx, by) for d in range(3))
        flat = vals.reshape(BX * BY, LANES)
        own = rim = None
        for w in range(4):
            s = c + (w - 1)
            inside = jnp.logical_and(lane2 >= s, lane2 < LANES + s)
            term = wz[w] * pltpu.roll(flat, lax.rem(LANES + s, LANES), 1)
            o, r = jnp.where(inside, term, 0.0), jnp.where(inside, 0.0, term)
            own, rim = (o, r) if own is None else (own + o, rim + r)
        YP[0:BX, 2 * HY:2 * HY + BY, :] = own.reshape(BX, BY, LANES)
        YP[BX:2 * BX, 2 * HY:2 * HY + BY, :] = rim.reshape(BX, BY, LANES)
        t = sum(wy[v] * YP[:, pl.ds((HY + 1 - v) - b, WY), :] for v in range(4))
        y0 = by * BY if isinstance(by, int) else pl.multiple_of(by * BY, BY)
        x0 = bx * BX
        for i, ref in enumerate((ACC, BU)):
            for m in range(BX + 3):
                XP[i, 2 * HX + m] = sum(wx[u] * t[i * BX + m - u] for u in range(4) if 0 <= m - u < BX)
            here = (pl.ds(x0, WX), pl.ds(y0, WY), slice(None))
            ref[here] = ref[here] + XP[i, pl.ds((HX + 1) - a, WX)]

    def pack_rims(ACC):
        for g in range(EG):
            for side in range(2):
                row = None
                for j in range(PK):
                    turned = pltpu.roll(BU[PK * g + j], (HZ * j + HZ * side) % LANES, 1)
                    row = turned if row is None else jnp.where(lane2 // HZ == j, turned, row)
                ACC[(EX + EG if side == 0 else EX) + g] = row

    def return_exchange(ACC, k, between):
        copies = []
        for n, way in enumerate(WAYS):
            copies.append((way, back[n].at[k], Copy(
                rim(ACC, way[2], region(way, piece)), back[n].at[k], way).start()))
        between()
        SUM[...] = jnp.zeros_like(SUM)
        for way, came, copy in copies:
            copy.landed()
            other = tuple(-w for w in way)
            xs, ys = region(other, border)
            if way[2]:
                side = 0 if way[2] > 0 else 1
                SUM[side, xs, ys, :] = SUM[side, xs, ys, :] + came[...]
            else:
                ACC[xs, ys, :] = ACC[xs, ys, :] + came[...]
        for g in range(G):
            first, last = SUM[0, XG + g, OY, :], SUM[1, XG + g, OY, :]
            for j in range(PK):
                x = PK * g + j
                turned = jnp.where(lane2 < HZ, pltpu.roll(first, (LANES - HZ * j) % LANES, 1),
                                   pltpu.roll(last, (LANES - HZ - HZ * j) % LANES, 1))
                edge = jnp.logical_or(lane2 < HZ, lane2 >= LANES - HZ)
                ADJ[x] = ACC[HX + x, OY, :] + jnp.where(edge, turned, 0.0)

    def each_block(fn):
        def step(n, carry):
            fn(n // NBY, n % NBY)
            return carry
        lax.fori_loop(0, NBX * NBY, step, 0)

    E0[OX, OY, :] = STEP_SIZE * sum(grad[0, c].astype(jnp.float32) * vel[c] for c in range(3))
    pack_own(E0, 0)
    pl.semaphore_wait(barrier, total)

    def prepare():
        for ref in (YP, XP, ACC0, ACC1, BU):
            ref[...] = jnp.zeros_like(ref)
        send_faces()

    def nothing():
        pass

    faces = []

    def send_faces():
        VE[:, LH:LH + TX, OY, :] = vel[...]
        for c in range(3):
            for i in range(TX // 2):
                for h in range(2):
                    YSU[c, i, LH * h:LH * (h + 1), :] = vel[c, 2 * i + h, TY - LH:TY, :]
                    YSD[c, i, LH * h:LH * (h + 1), :] = vel[c, 2 * i + h, 0:LH, :]
            for g in range(TX // VPK):
                row = None
                for j in range(VPK):
                    turned = pltpu.roll(vel[c, VPK * g + j], (2 * LH * j + LH) % LANES, 1)
                    row = turned if row is None else jnp.where(lane2 // (2 * LH) == j, turned, row)
                SV[c, g] = row
        faces.extend([
            Copy(SV, VRD, (0, 0, 1)).start(), Copy(SV, VRU, (0, 0, -1)).start(),
            Copy(vel.at[:, TX - LH:TX], VE.at[:, 0:LH, OY, :], (1, 0, 0)).start(),
            Copy(vel.at[:, 0:LH], VE.at[:, LH + TX:2 * LH + TX, OY, :], (-1, 0, 0)).start(),
            Copy(YSU, YVD, (0, 1, 0)).start(), Copy(YSD, YVU, (0, -1, 0)).start()])

    forward_exchange(E0, 0, prepare)
    unpack(E0)

    def first(bx, by):
        y0 = pl.multiple_of(by * BY, BY)
        ST[pl.ds(bx * BX, BX), pl.ds(y0, BY), :] = gather_block(E0, 0, bx, by)

    each_block(first)
    g1 = sum(grad[1, c].astype(jnp.float32) * vel[c] for c in range(3))
    E1[OX, OY, :] = ST[...] + STEP_SIZE * g1
    pack_own(E1, 1)

    forward_exchange(E1, 1, nothing)
    unpack(E1)

    def second(bx, by):
        spread_block(ACC1, gather_block(E1, 1, bx, by), 1, bx, by)

    each_block(second)
    pack_rims(ACC1)

    def regular():
        for f in faces:
            f.landed()
        for c in range(3):
            for i in range(TX // 2):
                for h in range(2):
                    VE[c, LH + 2 * i + h, HY - LH:HY, :] = YVD[c, i, LH * h:LH * (h + 1), :]
                    VE[c, LH + 2 * i + h, HY + TY:HY + TY + LH, :] = YVU[c, i, LH * h:LH * (h + 1), :]
        rows = lax.broadcasted_iota(jnp.int32, (2 * LANES, LANES), 0)
        cols = lax.broadcasted_iota(jnp.int32, (2 * LANES, LANES), 1)
        r = rows - LANES
        place = jnp.where(rows < LANES, rows, jnp.where(r < LH, r + LANES, r - LANES))
        known = jnp.logical_or(rows < LANES, jnp.logical_or(r < LH, r >= LANES - LH))
        gap = jnp.abs(place - cols)
        band = jnp.zeros((2 * LANES, LANES), jnp.float32)
        for k in range(5):
            tap = (3.0 if k == 0 else 1.0) * LAPLACE_TAPS[k]
            band = jnp.where(jnp.logical_and(known, gap == k), tap, band)
        for c in range(3):
            rims = []
            for g in range(TX // VPK):
                row = jnp.where(lane2 % (2 * LH) < LH, VRD[c, g], VRU[c, g])
                for j in range(VPK):
                    rims.append(pltpu.roll(row, (LANES - (2 * LH * j + LH)) % LANES, 1))
            rim = jnp.concatenate(rims, axis=0)
            own = vel[c].reshape(TX * TY, LANES)
            res = jnp.dot(jnp.concatenate([own, rim], axis=1), band,
                          preferred_element_type=jnp.float32,
                          precision=lax.Precision.HIGHEST).reshape(TX, TY, LANES)
            for k in range(1, 5):
                res = res + LAPLACE_TAPS[k] * (
                    VE[c, LH + k:LH + k + TX, OY, :] + VE[c, LH - k:LH - k + TX, OY, :]
                    + VE[c, LH:LH + TX, HY + k:HY + k + TY, :]
                    + VE[c, LH:LH + TX, HY - k:HY - k + TY, :])
            out[c] = (-REG_WEIGHT) * res

    return_exchange(ACC1, 1, regular)

    def third(bx, by):
        y0 = pl.multiple_of(by * BY, BY)
        vals = ADJ[pl.ds(bx * BX, BX), pl.ds(y0, BY), :]
        spread_block(ACC0, vals, 0, bx, by)

    BU[...] = jnp.zeros_like(BU)
    each_block(third)
    pack_rims(ACC0)

    def add_gauss(k):
        for c in range(3):
            out[c] = out[c] + STEP_SIZE * grad[k, c].astype(jnp.float32) * ADJ[...]

    return_exchange(ACC0, 0, functools.partial(add_gauss, 1))
    add_gauss(0)
    for copy in sends:
        copy.left()


COPIES = 4 * len(WAYS) + 6


def body(shape, velocity, gradients, shift_x, shift_y, shift_z, fractions):
    TX, TY, TZ = velocity.shape[1:]
    assert TZ == BZ == LANES and TX % VPK == 0 and TX % BX == 0 and TY % BY == 0
    EX, EY = TX + 2 * HX, TY + 2 * HY
    EG, G = EX // PK, TX // PK

    def span(way):
        groups = (XG if way[0] else G) if way[2] else (HX if way[0] else TX)
        return groups, HY if way[1] else TY

    vm = lambda *s: pltpu.VMEM(s, jnp.float32)
    vmem = pl.BlockSpec(memory_space=pltpu.VMEM)
    smem = pl.BlockSpec(memory_space=pltpu.SMEM)
    shift_x, shift_y, shift_z = (s.transpose(0, 1, 3, 2) for s in (shift_x, shift_y, shift_z))
    fractions = fractions.transpose(0, 2, 3, 4, 1)
    return pl.pallas_call(
        functools.partial(kernel, shape),
        out_shape=jax.ShapeDtypeStruct(velocity.shape, jnp.float32),
        in_specs=[vmem, vmem, smem, smem, smem, smem],
        out_specs=vmem,
        scratch_shapes=[
            vm(EX + 2 * EG, EY, LANES), vm(EX + 2 * EG, EY, LANES),
            vm(EX, EY, LANES), vm(2 * BX, WY, LANES),
            vm(2 * BX, 2 * WY - BY, LANES), vm(2, 2 * WX - BX, WY, LANES),
            vm(EX + 2 * EG, EY, LANES), vm(EX + 2 * EG, EY, LANES),
            vm(EX, EY, LANES), vm(TX, TY, LANES), vm(TX, TY, LANES),
            vm(2, 2, EG, EY, LANES), vm(2, EG, EY, LANES),
            vm(3, TX + 2 * LH, EY, LANES),
            vm(3, TX // 2, 2 * LH, LANES), vm(3, TX // 2, 2 * LH, LANES),
            vm(3, TX // 2, 2 * LH, LANES), vm(3, TX // 2, 2 * LH, LANES),
            vm(3, TX // VPK, TY, LANES), vm(3, TX // VPK, TY, LANES), vm(3, TX // VPK, TY, LANES),
            *[vm(2, *span(way), LANES) for way in WAYS],
            pltpu.SemaphoreType.DMA((COPIES,)), pltpu.SemaphoreType.DMA((COPIES,)),
        ],
        compiler_params=pltpu.CompilerParams(collective_id=0, has_side_effects=True,
                                             vmem_limit_bytes=16 << 20),
    )(velocity, gradients, shift_x, shift_y, shift_z, fractions)


def solution(mesh):
    in_specs = (
        P(None, "gx", "gy", "gz"),
        P(None, None, "gx", "gy", "gz"),
        P(None, "gx", "gy", "gz"),
        P(None, "gx", "gy", "gz"),
        P(None, "gx", "gy", "gz"),
        P(None, None, "gx", "gy", "gz"),
    )
    out_specs = P(None, "gx", "gy", "gz")
    return jax.shard_map(functools.partial(body, dict(mesh.shape)), mesh=mesh, in_specs=in_specs,
                         out_specs=out_specs, check_vma=False)
```

time: 46.7 us -> 36.7 us (0.79); the launches traced: 45.8 us -> 36.4 us
  Pallas kernels: 40.5 us -> 31.6 us
  local copies, waits for them, and re-layouts: 5.27 us -> 4.8 us
    pallas_call x1, Pallas kernels: 40.5 us -> 31.6 us  [body(): pl.pallas_call(functools.partial(kernel, shape), out_shape=jax.ShapeDtype...]
    unnamed x11 -> x13, local copies, waits for them, and re-layouts: 5.27 us -> 4.8 us
where the time goes in v2:
time: 36.7 us; the launch traced here: 36.4 us
  Pallas kernels  31.6 us (86%)
  local copies, waits for them, and re-layouts  4.8 us (13%)
    pallas_call x1, Pallas kernels, body(): pl.pallas_call(functools.partial(kernel, shape), out_shape=jax.ShapeDtype...  31.6 us
    unnamed x13, local copies, waits for them, and re-layouts  4.8 us

profile of v2, /device:TPU:0, one launch (start us, length us, event | category | flops | bytes accessed | tf_op | source)
XLA Modules:
  0.0 36.4 jit_solution(13138871429449834078)
XLA Ops:
  0.0 0.0 copy-start.2
  0.0 0.0 copy-start.3
  0.0 0.7 %copy-done.2 = s32[2,3,2,2,1]{1,4,3,2,0:T(1,128)S(1)} copy-done((s32[2,3,2,2,1]{1,4,3,2,0:T(1,128)S(1)}, s32[2,3,2,2,1]{1,4,3,2,0:T(1,128)}, u32[]{:S(2)}) %copy-start.2) | copy-done | bytes 120
  0.7 0.0 copy-done.3
  0.7 0.0 copy-start
  0.7 1.0 %copy-done = f32[3,16,16,128]{3,2,1,0:T(8,128)S(1)} copy-done((f32[3,16,16,128]{3,2,1,0:T(8,128)S(1)}, f32[3,16,16,128]{3,2,1,0:T(8,128)}, u32[]{:S(2)}) %copy-start) | copy-done | bytes 393240
  1.7 0.0 copy-start.1
  1.7 1.0 %copy-done.1 = bf16[2,3,16,16,128]{4,3,2,1,0:T(8,128)(2,1)S(1)} copy-done((bf16[2,3,16,16,128]{4,3,2,1,0:T(8,128)(2,1)S(1)}, bf16[2,3,16,16,128]{4,3,2,1,0:T(8,128)(2,1)}, u32[]{:S(2)}) %copy-start.1) | copy-done | bytes 393240
  2.7 0.0 copy-start.4
  2.7 0.7 %copy-done.4 = s32[2,2,2,1]{2,3,1,0:T(1,128)S(1)} copy-done((s32[2,2,2,1]{2,3,1,0:T(1,128)S(1)}, s32[2,2,2,1]{2,3,1,0:T(1,128)}, u32[]{:S(2)}) %copy-start.4) | copy-done | bytes 56
  3.4 0.0 copy-start.5
  3.4 0.7 %copy-done.5 = s32[2,2,2,1]{2,3,1,0:T(1,128)S(1)} copy-done((s32[2,2,2,1]{2,3,1,0:T(1,128)S(1)}, s32[2,2,2,1]{2,3,1,0:T(1,128)}, u32[]{:S(2)}) %copy-start.5) | copy-done | bytes 56
  4.1 31.6 %shard_map.64 = f32[3,16,16,128]{3,2,1,0:T(8,128)S(1)} custom-call(f32[3,16,16,128]{3,2,1,0:T(8,128)S(1)} %copy-done, bf16[2,3,16,16,128]{4,3,2,1,0:T(8,128)(2,1)S(1)} %copy-done.1, s32[2,2,1,2]{3,2,1,0:T(1,128)S(1)} %bitcast.11, s32[2,2,1,2]{3,2,1,0:T(1,128)S(1)} %bitcast.12, s32[2,2,1,2]{3,2,1,0:T(1,128)S(1)} %bitcast.13, s32[2,2,2,1,3]{4,3,2,1,0:T(1,128)S(1)} %bitcast.10), custom_call_target="tpu_custom_call" | custom-call | tf_op jit(solution)/shard_map/pallas_call | solution.py:363
  35.7 0.7 %copy.11 = f32[3,16,16,128]{3,2,1,0:T(8,128)} copy(f32[3,16,16,128]{3,2,1,0:T(8,128)S(1)} %shard_map.64) | data formatting | bytes 786432
Async XLA Ops:
  0.0 0.7 %copy-start.2 = (s32[2,3,2,2,1]{1,4,3,2,0:T(1,128)S(1)}, s32[2,3,2,2,1]{1,4,3,2,0:T(1,128)}, u32[]{:S(2)}) copy-start(s32[2,3,2,2,1]{1,4,3,2,0:T(1,128)} %param.11) | copy-start | bytes 292
  0.0 0.7 %copy-start.3 = (s32[2,2,2,1]{2,3,1,0:T(1,128)S(1)}, s32[2,2,2,1]{2,3,1,0:T(1,128)}, u32[]{:S(2)}) copy-start(s32[2,2,2,1]{2,3,1,0:T(1,128)} %param.8) | copy-start | bytes 100
  0.7 1.0 %copy-start = (f32[3,16,16,128]{3,2,1,0:T(8,128)S(1)}, f32[3,16,16,128]{3,2,1,0:T(8,128)}, u32[]{:S(2)}) copy-start(f32[3,16,16,128]{3,2,1,0:T(8,128)} %vel.1) | copy-start | bytes 1179652
  1.7 1.0 %copy-start.1 = (bf16[2,3,16,16,128]{4,3,2,1,0:T(8,128)(2,1)S(1)}, bf16[2,3,16,16,128]{4,3,2,1,0:T(8,128)(2,1)}, u32[]{:S(2)}) copy-start(bf16[2,3,16,16,128]{4,3,2,1,0:T(8,128)(2,1)} %grad.1) | copy-start | bytes 1179652
  2.7 0.7 %copy-start.4 = (s32[2,2,2,1]{2,3,1,0:T(1,128)S(1)}, s32[2,2,2,1]{2,3,1,0:T(1,128)}, u32[]{:S(2)}) copy-start(s32[2,2,2,1]{2,3,1,0:T(1,128)} %param.9) | copy-start | bytes 100
  3.4 0.7 %copy-start.5 = (s32[2,2,2,1]{2,3,1,0:T(1,128)S(1)}, s32[2,2,2,1]{2,3,1,0:T(1,128)}, u32[]{:S(2)}) copy-start(s32[2,2,2,1]{2,3,1,0:T(1,128)} %param.10) | copy-start | bytes 100

commit v3 on v2

--- a/solution.py
+++ b/solution.py
@@ -43,8 +43,9 @@
     return {-1: (halo, 2 * halo), 0: (halo, halo + own), 1: (own, halo + own)}[way]
 
 
-def kernel(shape, vel, grad, shx, shy, shz, frac, out,
-           E0, E1, U, T, YP, XP, ACC0, ACC1, BU, ST, ADJ, SP, SUM,
+def kernel(shape, vel_in, grad_in, shx_in, shy_in, shz_in, frac_in, out,
+           vel, grad, shx, shy, shz, frac, arrive,
+           E0, E1, U, YP, XP, ACC0, ACC1, T, ST, ADJ, SP, SUM,
            VE, YSU, YSD, YVD, YVU, SV, VRD, VRU, *rest):
     back, (send, recv) = rest[:-2], rest[-2:]
     TX, TY, TZ = vel.shape[1:]
@@ -68,6 +69,11 @@
     def device(way):
         return {a: at[a] + w for a, w in zip(AXES, way) if w}
 
+    loads = [pltpu.make_async_copy(a, b, arrive.at[n]) for n, (a, b) in enumerate((
+        (vel_in, vel), (grad_in, grad), (shx_in, shx), (shy_in, shy), (shz_in, shz), (frac_in, frac)))]
+    for load in loads:
+        load.start()
+
     sends = []
 
     class Copy:
@@ -103,14 +109,25 @@
             pl.semaphore_signal(barrier, inc=1, device_id=device(way), device_id_type=MESH)
         total = total + has(way).astype(jnp.int32)
 
+    group = lane2 // HZ
+
+    def packed(layer, g):
+        first = last = None
+        for j in range(PK):
+            turned = pltpu.roll(layer(PK * g + j), HZ * j, 1) if j else layer(PK * g)
+            first = turned if j == 0 else jnp.where(group == j, turned, first)
+            last = turned if j == 0 else jnp.where(group == j - 1, turned, last)
+        return first, last
+
+    def unpacked(first, last, j):
+        both = jnp.where(group == j, first, last)
+        return pltpu.roll(both, LANES - HZ * j, 1) if j else both
+
     def pack_own(E, k):
+        def layer(x):
+            return E[HX + x, OY, :]
         for g in range(G):
-            for side in range(2):
-                row = None
-                for j in range(PK):
-                    turned = pltpu.roll(E[HX + PK * g + j, OY, :], (HZ * j + HZ * side) % LANES, 1)
-                    row = turned if row is None else jnp.where(lane2 // HZ == j, turned, row)
-                SP[k, side, HX // PK + g, OY, :] = row
+            SP[k, 0, XG + g, OY, :], SP[k, 1, XG + g, OY, :] = packed(layer, g)
 
     def region(way, dim_of):
         (x0, x1) = dim_of(way[0], G if way[2] else TX, XG if way[2] else HX)
@@ -140,9 +157,7 @@
         for g in range(EG):
             below, above = E[EX + g], E[EX + EG + g]
             for j in range(PK):
-                U[PK * g + j] = jnp.where(
-                    lane2 < HZ, pltpu.roll(above, (LANES - HZ * j) % LANES, 1),
-                    pltpu.roll(below, (LANES - HZ - HZ * j) % LANES, 1))
+                U[PK * g + j] = unpacked(above, below, j)
 
     def taps(k, d, bx, by):
         e = frac[k, bx, by, 0, d].astype(jnp.float32) * 0.125
@@ -152,14 +167,15 @@
                 0.5 * (4.0 * e2 - 3.0 * e3 + e), 0.5 * (e3 - e2))
 
     def gather_block(E, k, bx, by):
+        n = bx * NBY + by
         a, b, c = shx[k, bx, 0, by], shy[k, bx, 0, by], shz[k, bx, 0, by]
         wx, wy, wz = (taps(k, d, bx, by) for d in range(3))
-        y0 = by * BY if isinstance(by, int) else pl.multiple_of(by * BY, BY)
+        y0 = by * BY
         x0 = bx * BX + (a + HX - 1)
         for i, ref in enumerate((E, U)):
             win = ref[pl.ds(x0, BX + 3), pl.ds(y0, WY), :]
-            T[i * BX:(i + 1) * BX] = sum(wx[u] * win[u:u + BX] for u in range(4))
-        y = sum(wy[v] * T[:, pl.ds(b + (HY - 1 + v), BY), :] for v in range(4))
+            T[n, i * BX:(i + 1) * BX] = sum(wx[u] * win[u:u + BX] for u in range(4))
+        y = sum(wy[v] * T[n, :, pl.ds(b + (HY - 1 + v), BY), :] for v in range(4))
         own, rim = y[:BX].reshape(BX * BY, LANES), y[BX:].reshape(BX * BY, LANES)
         res = None
         for w in range(4):
@@ -169,7 +185,8 @@
             res = term if res is None else res + term
         return res.reshape(BX, BY, LANES)
 
-    def spread_block(ACC, vals, k, bx, by):
+    def spread_block(vals, k, bx, by):
+        n = bx * NBY + by
         a, b, c = shx[k, bx, 0, by], shy[k, bx, 0, by], shz[k, bx, 0, by]
         wx, wy, wz = (taps(k, d, bx, by) for d in range(3))
         flat = vals.reshape(BX * BY, LANES)
@@ -180,25 +197,35 @@
             term = wz[w] * pltpu.roll(flat, lax.rem(LANES + s, LANES), 1)
             o, r = jnp.where(inside, term, 0.0), jnp.where(inside, 0.0, term)
             own, rim = (o, r) if own is None else (own + o, rim + r)
-        YP[0:BX, 2 * HY:2 * HY + BY, :] = own.reshape(BX, BY, LANES)
-        YP[BX:2 * BX, 2 * HY:2 * HY + BY, :] = rim.reshape(BX, BY, LANES)
-        t = sum(wy[v] * YP[:, pl.ds((HY + 1 - v) - b, WY), :] for v in range(4))
-        y0 = by * BY if isinstance(by, int) else pl.multiple_of(by * BY, BY)
-        x0 = bx * BX
-        for i, ref in enumerate((ACC, BU)):
+        YP[n, 0:BX, 2 * HY:2 * HY + BY, :] = own.reshape(BX, BY, LANES)
+        YP[n, BX:2 * BX, 2 * HY:2 * HY + BY, :] = rim.reshape(BX, BY, LANES)
+        t = sum(wy[v] * YP[n, :, pl.ds((HY + 1 - v) - b, WY), :] for v in range(4))
+        for i in range(2):
             for m in range(BX + 3):
-                XP[i, 2 * HX + m] = sum(wx[u] * t[i * BX + m - u] for u in range(4) if 0 <= m - u < BX)
-            here = (pl.ds(x0, WX), pl.ds(y0, WY), slice(None))
-            ref[here] = ref[here] + XP[i, pl.ds((HX + 1) - a, WX)]
-
-    def pack_rims(ACC):
+                XP[n, i, 2 * HX + m] = sum(wx[u] * t[i * BX + m - u] for u in range(4) if 0 <= m - u < BX)
+
+    def collect(ACC, k):
+        starts = {(bx, by): (HX + 1) - shx[k, bx, 0, by] for bx in range(NBX) for by in range(NBY)}
+
+        def layer(i, x):
+            tiles = [None] * ((TY + 2 * HY) // BY)
+            for bx in range(NBX):
+                if not 0 <= x - bx * BX < WX:
+                    continue
+                for by in range(NBY):
+                    rows = XP[bx * NBY + by, i, starts[bx, by] + (x - bx * BX)]
+                    for q in range(WY // BY):
+                        part = rows[q * BY:(q + 1) * BY]
+                        old = tiles[by + q]
+                        tiles[by + q] = part if old is None else old + part
+            return jnp.concatenate(tiles, axis=0)
+
         for g in range(EG):
-            for side in range(2):
-                row = None
-                for j in range(PK):
-                    turned = pltpu.roll(BU[PK * g + j], (HZ * j + HZ * side) % LANES, 1)
-                    row = turned if row is None else jnp.where(lane2 // HZ == j, turned, row)
-                ACC[(EX + EG if side == 0 else EX) + g] = row
+            above, below = packed(functools.partial(layer, 1), g)
+            ACC[EX + EG + g] = above
+            ACC[EX + g] = below
+        for x in range(EX):
+            ACC[x] = layer(0, x)
 
     def return_exchange(ACC, k, between):
         copies = []
@@ -220,23 +247,22 @@
             first, last = SUM[0, XG + g, OY, :], SUM[1, XG + g, OY, :]
             for j in range(PK):
                 x = PK * g + j
-                turned = jnp.where(lane2 < HZ, pltpu.roll(first, (LANES - HZ * j) % LANES, 1),
-                                   pltpu.roll(last, (LANES - HZ - HZ * j) % LANES, 1))
                 edge = jnp.logical_or(lane2 < HZ, lane2 >= LANES - HZ)
-                ADJ[x] = ACC[HX + x, OY, :] + jnp.where(edge, turned, 0.0)
+                ADJ[x] = ACC[HX + x, OY, :] + jnp.where(edge, unpacked(first, last, j), 0.0)
 
     def each_block(fn):
-        def step(n, carry):
-            fn(n // NBY, n % NBY)
-            return carry
-        lax.fori_loop(0, NBX * NBY, step, 0)
-
+        for bx in range(NBX):
+            for by in range(NBY):
+                fn(bx, by)
+
+    for load in loads:
+        load.wait()
     E0[OX, OY, :] = STEP_SIZE * sum(grad[0, c].astype(jnp.float32) * vel[c] for c in range(3))
     pack_own(E0, 0)
     pl.semaphore_wait(barrier, total)
 
     def prepare():
-        for ref in (YP, XP, ACC0, ACC1, BU):
+        for ref in (YP, XP):
             ref[...] = jnp.zeros_like(ref)
         send_faces()
 
@@ -268,7 +294,7 @@
     unpack(E0)
 
     def first(bx, by):
-        y0 = pl.multiple_of(by * BY, BY)
+        y0 = by * BY
         ST[pl.ds(bx * BX, BX), pl.ds(y0, BY), :] = gather_block(E0, 0, bx, by)
 
     each_block(first)
@@ -280,10 +306,10 @@
     unpack(E1)
 
     def second(bx, by):
-        spread_block(ACC1, gather_block(E1, 1, bx, by), 1, bx, by)
+        spread_block(gather_block(E1, 1, bx, by), 1, bx, by)
 
     each_block(second)
-    pack_rims(ACC1)
+    collect(ACC1, 1)
 
     def regular():
         for f in faces:
@@ -324,22 +350,24 @@
     return_exchange(ACC1, 1, regular)
 
     def third(bx, by):
-        y0 = pl.multiple_of(by * BY, BY)
+        y0 = by * BY
         vals = ADJ[pl.ds(bx * BX, BX), pl.ds(y0, BY), :]
-        spread_block(ACC0, vals, 0, bx, by)
-
-    BU[...] = jnp.zeros_like(BU)
+        spread_block(vals, 0, bx, by)
+
     each_block(third)
-    pack_rims(ACC0)
+    collect(ACC0, 0)
 
     def add_gauss(k):
         for c in range(3):
             out[c] = out[c] + STEP_SIZE * grad[k, c].astype(jnp.float32) * ADJ[...]
 
-    return_exchange(ACC0, 0, functools.partial(add_gauss, 1))
+    def last():
+        add_gauss(1)
+        for copy in sends:
+            copy.left()
+
+    return_exchange(ACC0, 0, last)
     add_gauss(0)
-    for copy in sends:
-        copy.left()
 
 
 COPIES = 4 * len(WAYS) + 6
@@ -350,6 +378,7 @@
     assert TZ == BZ == LANES and TX % VPK == 0 and TX % BX == 0 and TY % BY == 0
     EX, EY = TX + 2 * HX, TY + 2 * HY
     EG, G = EX // PK, TX // PK
+    NB = (TX // BX) * (TY // BY)
 
     def span(way):
         groups = (XG if way[0] else G) if way[2] else (HX if way[0] else TX)
@@ -357,20 +386,23 @@
 
     vm = lambda *s: pltpu.VMEM(s, jnp.float32)
     vmem = pl.BlockSpec(memory_space=pltpu.VMEM)
-    smem = pl.BlockSpec(memory_space=pltpu.SMEM)
+    hbm = pl.BlockSpec(memory_space=pltpu.HBM)
     shift_x, shift_y, shift_z = (s.transpose(0, 1, 3, 2) for s in (shift_x, shift_y, shift_z))
     fractions = fractions.transpose(0, 2, 3, 4, 1)
     return pl.pallas_call(
         functools.partial(kernel, shape),
         out_shape=jax.ShapeDtypeStruct(velocity.shape, jnp.float32),
-        in_specs=[vmem, vmem, smem, smem, smem, smem],
+        in_specs=[hbm] * 6,
         out_specs=vmem,
         scratch_shapes=[
+            pltpu.VMEM(velocity.shape, velocity.dtype), pltpu.VMEM(gradients.shape, gradients.dtype),
+            *[pltpu.SMEM(s.shape, s.dtype) for s in (shift_x, shift_y, shift_z, fractions)],
+            pltpu.SemaphoreType.DMA((6,)),
             vm(EX + 2 * EG, EY, LANES), vm(EX + 2 * EG, EY, LANES),
-            vm(EX, EY, LANES), vm(2 * BX, WY, LANES),
-            vm(2 * BX, 2 * WY - BY, LANES), vm(2, 2 * WX - BX, WY, LANES),
+            vm(EX, EY, LANES),
+            vm(NB, 2 * BX, 2 * WY - BY, LANES), vm(NB, 2, 2 * WX - BX, WY, LANES),
             vm(EX + 2 * EG, EY, LANES), vm(EX + 2 * EG, EY, LANES),
-            vm(EX, EY, LANES), vm(TX, TY, LANES), vm(TX, TY, LANES),
+            vm(NB, 2 * BX, WY, LANES), vm(TX, TY, LANES), vm(TX, TY, LANES),
             vm(2, 2, EG, EY, LANES), vm(2, EG, EY, LANES),
             vm(3, TX + 2 * LH, EY, LANES),
             vm(3, TX // 2, 2 * LH, LANES), vm(3, TX // 2, 2 * LH, LANES),
@@ -380,7 +412,7 @@
             pltpu.SemaphoreType.DMA((COPIES,)), pltpu.SemaphoreType.DMA((COPIES,)),
         ],
         compiler_params=pltpu.CompilerParams(collective_id=0, has_side_effects=True,
-                                             vmem_limit_bytes=16 << 20),
+                                             vmem_limit_bytes=60 * 1024 * 1024),
     )(velocity, gradients, shift_x, shift_y, shift_z, fractions)
 
 

time: 36.7 us -> 31.6 us (0.86)
  local copies, waits for them, and re-layouts: 4.8 us -> 1.77 us
  Pallas kernels: 31.6 us -> 29.6 us
    unnamed x13 -> x1, local copies, waits for them, and re-layouts: 4.8 us -> 1.77 us
    pallas_call x1, Pallas kernels: 31.6 us -> 29.6 us  [body(): pl.pallas_call(functools.partial(kernel, shape), out_shape=jax.ShapeDtype...]
where the time goes in v3:
time: 31.6 us; the launch traced here: 31.4 us
  Pallas kernels  29.6 us (94%)
  local copies, waits for them, and re-layouts  1.77 us (6%)
    pallas_call x1, Pallas kernels, body(): pl.pallas_call(functools.partial(kernel, shape), out_shape=jax.ShapeDtype...  29.6 us
    unnamed x1, local copies, waits for them, and re-layouts  1.77 us

profile of v3, /device:TPU:0, one launch (start us, length us, event | category | flops | bytes accessed | tf_op | source)
XLA Modules:
  0.0 31.4 jit_solution(1974042151744595756)
XLA Ops:
  0.0 29.6 %shard_map.64 = f32[3,16,16,128]{3,2,1,0:T(8,128)} custom-call(f32[3,16,16,128]{3,2,1,0:T(8,128)} %vel_in.1, bf16[2,3,16,16,128]{4,3,2,1,0:T(8,128)(2,1)} %grad_in.1, s32[2,2,1,2]{3,2,1,0:T(1,128)} %bitcast.11, s32[2,2,1,2]{3,2,1,0:T(1,128)} %bitcast.12, s32[2,2,1,2]{3,2,1,0:T(1,128)} %bitcast.13, s32[2,2,2,1,3]{4,3,2,1,0:T(1,128)} %bitcast.10), custom_call_target="tpu_custom_call" | custom-call | tf_op jit(solution)/shard_map/pallas_call | solution.py:392
  29.7 1.8 %copy.11 = f32[3,16,16,128]{3,2,1,0:T(8,128)} copy(f32[3,16,16,128]{3,2,1,0:T(8,128)} %shard_map.64) | data formatting | bytes 786432

commit v4 on v3

--- a/solution.py
+++ b/solution.py
@@ -412,8 +412,8 @@
             pltpu.SemaphoreType.DMA((COPIES,)), pltpu.SemaphoreType.DMA((COPIES,)),
         ],
         compiler_params=pltpu.CompilerParams(collective_id=0, has_side_effects=True,
-                                             vmem_limit_bytes=60 * 1024 * 1024),
-    )(velocity, gradients, shift_x, shift_y, shift_z, fractions)
+                                             vmem_limit_bytes=16 << 20),
+    )(*(pltpu.with_memory_space_constraint(x, pltpu.HBM) for x in (velocity, gradients, shift_x, shift_y, shift_z, fractions)))
 
 
 def solution(mesh):

time: 31.6 us -> 29.8 us (0.943)
  local copies, waits for them, and re-layouts: 1.77 us -> 0.75 us
  Pallas kernels: 29.6 us -> 28.9 us
    unnamed x1, local copies, waits for them, and re-layouts: 1.77 us -> 0.75 us
    pallas_call x1, Pallas kernels: 29.6 us -> 28.9 us  [body(): pl.pallas_call(functools.partial(kernel, shape), out_shape=jax.ShapeDtype...]
where the time goes in v4:
time: 29.8 us; the launch traced here: 29.7 us
  Pallas kernels  28.9 us (97%)
  local copies, waits for them, and re-layouts  0.75 us (3%)
    pallas_call x1, Pallas kernels, body(): pl.pallas_call(functools.partial(kernel, shape), out_shape=jax.ShapeDtype...  28.9 us
    unnamed x1, local copies, waits for them, and re-layouts  0.75 us

profile of v4, /device:TPU:0, one launch (start us, length us, event | category | flops | bytes accessed | tf_op | source)
XLA Modules:
  0.0 29.7 jit_solution(12661072024852208375)
XLA Ops:
  0.0 28.9 %shard_map.64 = f32[3,16,16,128]{3,2,1,0:T(8,128)S(1)} custom-call(f32[3,16,16,128]{3,2,1,0:T(8,128)} %vel_in.1, bf16[2,3,16,16,128]{4,3,2,1,0:T(8,128)(2,1)} %grad_in.1, s32[2,2,1,2]{3,2,1,0:T(1,128)} %bitcast.11, s32[2,2,1,2]{3,2,1,0:T(1,128)} %bitcast.12, s32[2,2,1,2]{3,2,1,0:T(1,128)} %bitcast.13, s32[2,2,2,1,3]{4,3,2,1,0:T(1,128)} %bitcast.10), custom_call_target="tpu_custom_call" | custom-call | tf_op jit(solution)/shard_map/pallas_call | solution.py:392
  28.9 0.7 %copy.11 = f32[3,16,16,128]{3,2,1,0:T(8,128)} copy(f32[3,16,16,128]{3,2,1,0:T(8,128)S(1)} %shard_map.64) | data formatting | bytes 786432
